TPU v7x, 512 devices: a whole 4x8x8 slice. The times are simulated.
512 devices in a mesh: tok: 128 (over z, y, core), head: 4 (over x).
Axes of the slice: x: 4, y: 8, z: 8, core: 2. Of those that a mesh axis runs over, the one named last changes fastest.
Arguments:
- tokens: bfloat16 [16384, 1536], P('tok'), may hold values from -6 to 6
- norm_gain: bfloat16 [1536], replicated, may hold values from 0.099609375 to 1.8984375
- w_query: bfloat16 [1536, 1536], P('tok', 'head')
- w_keyval: bfloat16 [1536, 256], P('tok')
- w_out: bfloat16 [1536, 1536], P('head', 'tok'), may hold values from -0.5 to 0.5
- segment_ids: int32 [16384], P('tok'), may hold values from 0 to 30, as said below
- lengths: int32 [31], replicated, may hold values from 128 to 1024, as said below
- member_prompt: int32 [384], P('head'), may hold values from 0 to 30
Outputs:
- mixed: bfloat16 [16384, 1536], P('tok', 'head')
- cycle_cache: bfloat16 [384, 1024, 256], P('head', 'tok')
Inputs may be any that keep to these rules, and one draw needn't show every extreme that they name: The prompts lie end to end in the order of lengths and their lengths sum to 16384; one prompt has exactly 1024 tokens and one exactly 128. `segment_ids`: segment_ids_t is the prompt that holds token t under lengths, so it never falls.
All inputs are finite; a program needn't handle non-finite values.
Results may differ from a plain program's by a relative error of at most 0.013.
Values may be sent and summed in bfloat16 or wider, within the bound.
No kernel may reach another device: no remote copies, remote signals or barrier semaphores. Data moves between devices by JAX's collectives and lax.ppermute only.
A program may use at most 64 MiB of HBM per device.

v0:
```python
import math

import jax
import jax.numpy as jnp
from jax import lax
from jax.sharding import PartitionSpec as P

HD = 128
WINDOW = 1024


def shifted(block, axis, distance):
    devices = range(lax.axis_size(axis))
    route = [(i - distance, i) for i in devices if i - distance in devices]
    return lax.ppermute(block, axis, route)


def rotate(values, positions):
    half_width = values.shape[-1] // 2
    frequency = 10000.0 ** (-(jnp.arange(half_width, dtype=jnp.float32) * 2.0 / values.shape[-1]))
    angles = positions.astype(jnp.float32)[:, None] * frequency[None, :]
    cosine = jnp.cos(angles)[:, None, :]
    sine_values = jnp.sin(angles)[:, None, :]
    front_half = values[..., :half_width]
    back_half = values[..., half_width:]
    return jnp.concatenate(
        [
            front_half * cosine - back_half * sine_values,
            back_half * cosine + front_half * sine_values,
        ],
        axis=-1,
    )


def lookup_table(segments, table):
    matches = segments[:, None] == jnp.arange(table.shape[0], dtype=jnp.int32)[None, :]
    return jnp.sum(jnp.where(matches, table[None, :], 0), axis=1)


def per_device(tokens, norm_gain, w_query, w_keyval, w_out, segment_ids, lengths, member_prompt):
    shard_rows = tokens.shape[0]
    heads_here = w_query.shape[1] // HD
    devices = lax.axis_size("tok")
    tok_index = lax.axis_index("tok")
    head_index = lax.axis_index("head")
    prompts = lengths.shape[0]
    prompt_ends = jnp.cumsum(lengths)
    starts = prompt_ends - lengths
    global_index = tok_index * shard_rows + jnp.arange(shard_rows, dtype=jnp.int32)
    positions = global_index - lookup_table(segment_ids, starts)
    widened = tokens.astype(jnp.float32)
    normed = (
        widened
        * lax.rsqrt(jnp.mean(widened * widened, axis=1, keepdims=True) + 1e-06)
        * norm_gain.astype(jnp.float32)
    ).astype(jnp.bfloat16)

    def add_rows(piece):
        return jnp.dot(normed, piece, preferred_element_type=jnp.float32)

    queries = add_rows(lax.all_gather(w_query, "tok", axis=0, tiled=True))
    queries = rotate(queries.reshape(shard_rows, heads_here, HD), positions).astype(jnp.bfloat16)
    keyval = add_rows(lax.all_gather(w_keyval, "tok", axis=0, tiled=True))
    rotated = rotate(keyval[:, None, :HD], positions)[:, 0]
    pairs = jnp.concatenate([rotated, keyval[:, HD:]], axis=1).astype(jnp.bfloat16)
    rim_shards = -(-WINDOW // shard_rows)
    rim_pairs = []
    rim_segments = []
    for distance in range(rim_shards, 0, -1):
        got_pairs, got_segments = shifted((pairs, segment_ids), "tok", distance)
        rim_pairs.append(got_pairs)
        rim_segments.append(got_segments)
    all_pairs = jnp.concatenate(rim_pairs + [pairs], axis=0)
    key_segments = jnp.concatenate(rim_segments + [segment_ids], axis=0)
    key_index = (tok_index - rim_shards) * shard_rows + jnp.arange(
        (rim_shards + 1) * shard_rows, dtype=jnp.int32
    )
    score_scale = 1.0 / math.sqrt(HD)
    outputs = []
    for head_slot in range(heads_here):
        query_head = queries[:, head_slot, :]
        scores = (
            jnp.einsum(
                "qd,kd->qk", query_head, all_pairs[:, :HD], preferred_element_type=jnp.float32
            )
            * score_scale
        )
        allowed = (key_segments[None, :] == segment_ids[:, None]) & (
            key_index[None, :] <= global_index[:, None]
        )
        allowed = (
            allowed
            & (key_index[None, :] > global_index[:, None] - WINDOW)
            & (key_index[None, :] >= 0)
        )
        scores = jnp.where(allowed, scores, -jnp.inf)
        largest = jnp.max(scores, axis=1, keepdims=True)
        weights = jnp.exp(scores - largest)
        total = jnp.sum(weights, axis=1, keepdims=True)
        probs = weights.astype(jnp.bfloat16)
        summed = jnp.dot(probs, all_pairs[:, HD:], preferred_element_type=jnp.float32)
        outputs.append((summed / total).astype(jnp.bfloat16))
    attention = jnp.concatenate(outputs, axis=1)
    quarter_cols = tokens.shape[1] // lax.axis_size("head")
    residual = lax.dynamic_slice_in_dim(tokens, head_index * quarter_cols, quarter_cols, 1).astype(
        jnp.float32
    )
    partial_out = jnp.dot(
        attention,
        lax.all_gather(w_out, "tok", axis=1, tiled=True),
        preferred_element_type=jnp.float32,
    )
    head_total = lax.psum_scatter(
        partial_out.astype(jnp.bfloat16), "head", scatter_dimension=1, tiled=True
    ).astype(jnp.float32)
    mixed = (residual + head_total).astype(jnp.bfloat16)
    slots_here = WINDOW // devices
    first_segment = jnp.sum((prompt_ends <= tok_index * shard_rows).astype(jnp.int32))
    slot_index = jnp.arange(WINDOW, dtype=jnp.int32)
    prompt_index = jnp.arange(prompts, dtype=jnp.int32)
    outgoing = []
    for local_seg in range(2):
        prompt_here = first_segment + local_seg
        matches = prompt_index == prompt_here
        prompt_size = jnp.sum(jnp.where(matches, lengths, 0))
        prompt_start = jnp.sum(jnp.where(matches, starts, 0))
        lowest = prompt_size - WINDOW
        places = lowest + jnp.mod(slot_index - lowest, WINDOW)
        local_rows = prompt_start + places - tok_index * shard_rows
        usable = (
            (prompt_here < prompts) & (places >= 0) & (local_rows >= 0) & (local_rows < shard_rows)
        )
        fetched = jnp.take(pairs, jnp.clip(local_rows, 0, shard_rows - 1), axis=0)
        kept = jnp.where(usable[:, None], fetched, jnp.zeros_like(fetched))
        outgoing.append(kept.reshape(devices, slots_here * 2 * HD))
    incoming = lax.all_to_all(jnp.stack(outgoing), "tok", split_axis=1, concat_axis=1, tiled=True)
    source_rows = jnp.arange(devices, dtype=jnp.int32) * shard_rows
    source_first = jnp.sum((prompt_ends[None, :] <= source_rows[:, None]).astype(jnp.int32), axis=1)
    owners = jnp.stack([source_first, source_first + 1]).reshape(-1)
    chooser = (owners[None, :] == prompt_index[:, None]).astype(jnp.bfloat16)
    slot_table = jnp.dot(
        chooser,
        incoming.reshape(2 * devices, slots_here * 2 * HD),
        preferred_element_type=jnp.float32,
    ).astype(jnp.bfloat16)
    member_pick = (member_prompt[:, None] == prompt_index[None, :]).astype(jnp.bfloat16)
    cycle_cache = jnp.dot(member_pick, slot_table, preferred_element_type=jnp.float32).astype(
        jnp.bfloat16
    )
    cycle_cache = cycle_cache.reshape(member_prompt.shape[0], slots_here, 2 * HD)
    return (mixed, cycle_cache)


def solution(mesh):
    return jax.shard_map(
        per_device,
        mesh=mesh,
        in_specs=(
            P("tok", None),
            P(),
            P("tok", "head"),
            P("tok", None),
            P("head", "tok"),
            P("tok"),
            P(),
            P("head"),
        ),
        out_specs=(P("tok", "head"), P("head", "tok", None)),
        check_vma=False,
    )
```

profile of v0, /device:TPU:1, one launch (start us, length us, event | category | flops | bytes accessed | tf_op | source)
XLA Modules:
  0.0 273.5 jit_solution(13498664107108925658)
XLA Ops:
  7.9 0.8 copy.40
  8.8 0.7 convert_element_type.65
  9.5 1.2 fusion.6
  10.7 59.4 %all-gather.1 = bf16[128,12,256]{2,1,0:T(8,128)(2,1)S(1)} all-gather(bf16[1,12,256]{2,1,0:T(8,128)(2,1)} %bitcast.50), channel_id=1, replica_groups=mesh['tok'=128,'head'=4] {'tok'}, dimensions={0}, use_global_device_ids=true | all-gather | bytes 792576 | tf_op jit(solution)/shard_map/all_gather | solution.py:63
  72.3 1.4 fusion.68
  74.0 5.8 %collective-permute-start.8 = (bf16[128,256]{0,1:T(8,128)(2,1)S(1)}, bf16[128,256]{0,1:T(8,128)(2,1)S(1)}, u32[]{:S(2)}, u32[]{:S(2)}) collective-permute-start(bf16[128,256]{0,1:T(8,128)(2,1)S(1)} %pad_maximum_fusion.1), channel_id=1, source_target_pairs={{0,32},{4,36},{8,40},{12,44},{16,48},{20,52},{24,56},{28,60},{32,6... | collective-permute-start | bytes 196616 | tf_op jit(solution)/shard_map/ppermute | solution.py:15
  79.8 3.8 %collective-permute-start.9 = (bf16[128,256]{0,1:T(8,128)(2,1)S(1)}, bf16[128,256]{0,1:T(8,128)(2,1)S(1)}, u32[]{:S(2)}, u32[]{:S(2)}) collective-permute-start(bf16[128,256]{0,1:T(8,128)(2,1)S(1)} %pad_maximum_fusion.1), channel_id=1, source_target_pairs={{0,28},{4,32},{8,36},{12,40},{16,44},{20,48},{24,52},{28,56},{32,6... | collective-permute-start | bytes 196616 | tf_op jit(solution)/shard_map/ppermute | solution.py:15
  83.6 4.5 %collective-permute-start.10 = (bf16[128,256]{0,1:T(8,128)(2,1)S(1)}, bf16[128,256]{0,1:T(8,128)(2,1)S(1)}, u32[]{:S(2)}, u32[]{:S(2)}) collective-permute-start(bf16[128,256]{0,1:T(8,128)(2,1)S(1)} %pad_maximum_fusion.1), channel_id=1, source_target_pairs={{0,24},{4,28},{8,32},{12,36},{16,40},{20,44},{24,48},{28,52},{32,5... | collective-permute-start | bytes 196616 | tf_op jit(solution)/shard_map/ppermute | solution.py:15
  88.1 3.3 %collective-permute-start.11 = (bf16[128,256]{0,1:T(8,128)(2,1)S(1)}, bf16[128,256]{0,1:T(8,128)(2,1)S(1)}, u32[]{:S(2)}, u32[]{:S(2)}) collective-permute-start(bf16[128,256]{0,1:T(8,128)(2,1)S(1)} %pad_maximum_fusion.1), channel_id=1, source_target_pairs={{0,20},{4,24},{8,28},{12,32},{16,36},{20,40},{24,44},{28,48},{32,5... | collective-permute-start | bytes 196616 | tf_op jit(solution)/shard_map/ppermute | solution.py:15
  91.5 3.4 %collective-permute-start = (s32[128]{0:T(128)S(1)}, s32[128]{0:T(128)S(1)}, u32[]{:S(2)}, u32[]{:S(2)}) collective-permute-start(s32[128]{0:T(128)S(1)} %copy-done.4), channel_id=1, source_target_pairs={{0,32},{4,36},{8,40},{12,44},{16,48},{20,52},{24,56},{28,60},{32,6... | collective-permute-start | bytes 1544 | tf_op jit(solution)/shard_map/ppermute | solution.py:15
  96.9 1.3 fusion.66
  98.2 3.9 %gather_fusion = bf16[1024,256]{1,0:T(8,128)(2,1)S(1)} fusion(bf16[128,256]{1,0:T(8,128)(2,1)S(1)} %copy.46, s32[1024]{0:T(1024)S(1)} %get-tuple-element.27), kind=kCustom, calls=%fused_computation.clone | custom fusion | bytes 1052672 | tf_op jit(solution)/shard_map/jit(_take)/gather | solution.py:133
  102.2 1.3 compare_and_fusion
  103.5 1.3 compare_and_fusion.2
  105.4 3.9 %gather_fusion.1 = bf16[1024,256]{1,0:T(8,128)(2,1)S(1)} fusion(bf16[128,256]{1,0:T(8,128)(2,1)S(1)} %copy.46, s32[1024]{0:T(1024)S(1)} %get-tuple-element.28), kind=kCustom, calls=%fused_computation.1.clone | custom fusion | bytes 1052672 | tf_op jit(solution)/shard_map/jit(_take)/gather | solution.py:133
  110.0 3.2 %pad_maximum_fusion = bf16[2,128,2048]{2,0,1:T(2,128)(2,1)} fusion(bf16[1,128,2048]{2,0,1:T(2,128)(2,1)S(1)} %stack_reshape.9, bf16[1,128,2048]{2,0,1:T(2,128)(2,1)S(1)} %stack_reshape.8), kind=kLoop, calls=%fused_computation.17 | loop fusion | flops 2097152 | bytes 2097152 | tf_op jit(solution)/shard_map/stack | solution.py:136
  113.2 10.2 %all-to-all-start = ((bf16[2,128,2048]{2,0,1:T(2,128)(2,1)}), bf16[2,128,2048]{2,0,1:T(2,128)(2,1)S(1)}, u32[]{:S(2)}, u32[]{:S(2)}) async-start(bf16[2,128,2048]{2,0,1:T(2,128)(2,1)} %pad_maximum_fusion), calls=%async_computation | async-start | bytes 2097152 | tf_op jit(solution)/shard_map/all_to_all | solution.py:136
  123.4 0.7 all-gather.8.cloned.1.call-update
  124.5 7.4 %collective-permute-start.1 = (s32[128]{0:T(128)S(1)}, s32[128]{0:T(128)S(1)}, u32[]{:S(2)}, u32[]{:S(2)}) collective-permute-start(s32[128]{0:T(128)S(1)} %copy-done.4), channel_id=1, source_target_pairs={{0,28},{4,32},{8,36},{12,40},{16,44},{20,48},{24,52},{28,56},{32,6... | collective-permute-start | bytes 1544 | tf_op jit(solution)/shard_map/ppermute | solution.py:15
  131.9 9.6 %collective-permute-done.1 = s32[128]{0:T(128)S(1)} collective-permute-done((s32[128]{0:T(128)S(1)}, s32[128]{0:T(128)S(1)}, u32[]{:S(2)}, u32[]{:S(2)}) %collective-permute-start.1) | collective-permute-done | bytes 544 | tf_op jit(solution)/shard_map/ppermute | solution.py:15
  141.6 8.5 %collective-permute-start.2 = (s32[128]{0:T(128)S(1)}, s32[128]{0:T(128)S(1)}, u32[]{:S(2)}, u32[]{:S(2)}) collective-permute-start(s32[128]{0:T(128)S(1)} %copy-done.4), channel_id=1, source_target_pairs={{0,24},{4,28},{8,32},{12,36},{16,40},{20,44},{24,48},{28,52},{32,5... | collective-permute-start | bytes 1544 | tf_op jit(solution)/shard_map/ppermute | solution.py:15
  150.1 0.7 collective-permute-done.2
  150.8 8.7 %collective-permute-start.3 = (s32[128]{0:T(128)S(1)}, s32[128]{0:T(128)S(1)}, u32[]{:S(2)}, u32[]{:S(2)}) collective-permute-start(s32[128]{0:T(128)S(1)} %copy-done.4), channel_id=1, source_target_pairs={{0,20},{4,24},{8,28},{12,32},{16,36},{20,40},{24,44},{28,48},{32,5... | collective-permute-start | bytes 1544 | tf_op jit(solution)/shard_map/ppermute | solution.py:15
  159.5 0.7 collective-permute-done.3
  160.2 5.6 %collective-permute-start.4 = (s32[128]{0:T(128)S(1)}, s32[128]{0:T(128)S(1)}, u32[]{:S(2)}, u32[]{:S(2)}) collective-permute-start(s32[128]{0:T(128)S(1)} %copy-done.4), channel_id=1, source_target_pairs={{0,16},{4,20},{8,24},{12,28},{16,32},{20,36},{24,40},{28,44},{32,4... | collective-permute-start | bytes 1544 | tf_op jit(solution)/shard_map/ppermute | solution.py:15
  165.8 0.7 collective-permute-done.4
  166.5 6.8 %collective-permute-start.5 = (s32[128]{0:T(128)S(1)}, s32[128]{0:T(128)S(1)}, u32[]{:S(2)}, u32[]{:S(2)}) collective-permute-start(s32[128]{0:T(128)S(1)} %copy-done.4), channel_id=1, source_target_pairs={{0,12},{4,16},{8,20},{12,24},{16,28},{20,32},{24,36},{28,40},{32,4... | collective-permute-start | bytes 1544 | tf_op jit(solution)/shard_map/ppermute | solution.py:15
  173.3 0.7 collective-permute-done.5
  174.0 3.4 %collective-permute-start.6 = (s32[128]{0:T(128)S(1)}, s32[128]{0:T(128)S(1)}, u32[]{:S(2)}, u32[]{:S(2)}) collective-permute-start(s32[128]{0:T(128)S(1)} %copy-done.4), channel_id=1, source_target_pairs={{0,8},{4,12},{8,16},{12,20},{16,24},{20,28},{24,32},{28,36},{32,40... | collective-permute-start | bytes 1544 | tf_op jit(solution)/shard_map/ppermute | solution.py:15
  177.4 0.7 collective-permute-done.6
  178.1 4.7 %collective-permute-start.7 = (s32[128]{0:T(128)S(1)}, s32[128]{0:T(128)S(1)}, u32[]{:S(2)}, u32[]{:S(2)}) collective-permute-start(s32[128]{0:T(128)S(1)} %copy-done.4), channel_id=1, source_target_pairs={{0,4},{4,8},{8,12},{12,16},{16,20},{20,24},{24,28},{28,32},{32,36}... | collective-permute-start | bytes 1544 | tf_op jit(solution)/shard_map/ppermute | solution.py:15
  183.5 7.2 %collective-permute-start.12 = (bf16[128,256]{0,1:T(8,128)(2,1)S(1)}, bf16[128,256]{0,1:T(8,128)(2,1)S(1)}, u32[]{:S(2)}, u32[]{:S(2)}) collective-permute-start(bf16[128,256]{0,1:T(8,128)(2,1)S(1)} %pad_maximum_fusion.1), channel_id=1, source_target_pairs={{0,16},{4,20},{8,24},{12,28},{16,32},{20,36},{24,40},{28,44},{32,4... | collective-permute-start | bytes 196616 | tf_op jit(solution)/shard_map/ppermute | solution.py:15
  190.8 8.6 %collective-permute-start.13 = (bf16[128,256]{0,1:T(8,128)(2,1)S(1)}, bf16[128,256]{0,1:T(8,128)(2,1)S(1)}, u32[]{:S(2)}, u32[]{:S(2)}) collective-permute-start(bf16[128,256]{0,1:T(8,128)(2,1)S(1)} %pad_maximum_fusion.1), channel_id=1, source_target_pairs={{0,12},{4,16},{8,20},{12,24},{16,28},{20,32},{24,36},{28,40},{32,4... | collective-permute-start | bytes 196616 | tf_op jit(solution)/shard_map/ppermute | solution.py:15
  200.0 1.3 collective-permute-start.14
  201.9 3.3 %collective-permute-start.15 = (bf16[128,256]{0,1:T(8,128)(2,1)S(1)}, bf16[128,256]{0,1:T(8,128)(2,1)S(1)}, u32[]{:S(2)}, u32[]{:S(2)}) collective-permute-start(bf16[128,256]{0,1:T(8,128)(2,1)S(1)} %pad_maximum_fusion.1), channel_id=1, source_target_pairs={{0,4},{4,8},{8,12},{12,16},{16,20},{20,24},{24,28},{28,32},{32,36}... | collective-permute-start | bytes 196616 | tf_op jit(solution)/shard_map/ppermute | solution.py:15
  209.7 2.3 reshape.265
  212.7 1.4 fusion.79
  214.3 2.1 fusion.78
  216.4 2.3 reshape.269
  218.7 1.3 fusion.11
  220.0 1.4 fusion.77
  221.6 1.3 fusion.3
  222.9 1.3 fusion.4
  224.2 1.3 fusion.5
  226.1 0.9 copy.53
  228.1 0.8 copy.55
  228.9 36.3 %reduce-scatter.4.cloned.1.call-done = bf16[384,128]{1,0:T(8,128)(2,1)} async-done(((bf16[1536,128]{1,0:T(8,128)(2,1)}), bf16[384,128]{1,0:T(8,128)(2,1)}) %reduce-scatter.4.cloned.1.call-update) | async-done | bytes 98320
  265.3 1.0 copy.54
  (82 shorter events, 14.3 us)
Async XLA Ops:
  7.2 202.6 %all-gather.6.cloned.1.call-start = ((), (), s32[]{:S(2)}) async-start(), calls=%async_computation.2 | async-start | bytes 1585152 | tf_op jit(solution)/shard_map/all_gather | solution.py:61
  70.1 1.0 copy-start
  70.1 2.2 copy-start.2
  70.1 3.6 %copy-start.4 = (s32[128]{0:T(128)S(1)}, s32[128]{0:T(128)}, u32[]{:S(2)}) copy-start(s32[128]{0:T(128)} %param.15) | copy-start | bytes 1540
  74.0 116.7 %collective-permute-start.8 = (bf16[128,256]{0,1:T(8,128)(2,1)S(1)}, bf16[128,256]{0,1:T(8,128)(2,1)S(1)}, u32[]{:S(2)}, u32[]{:S(2)}) collective-permute-start(bf16[128,256]{0,1:T(8,128)(2,1)S(1)} %pad_maximum_fusion.1), channel_id=1, source_target_pairs={{0,32},{4,36},{8,40},{12,44},{16,48},{20,52},{24,56},{28,60},{32,6... | collective-permute-start | bytes 196616 | tf_op jit(solution)/shard_map/ppermute | solution.py:15
  79.8 120.1 %collective-permute-start.9 = (bf16[128,256]{0,1:T(8,128)(2,1)S(1)}, bf16[128,256]{0,1:T(8,128)(2,1)S(1)}, u32[]{:S(2)}, u32[]{:S(2)}) collective-permute-start(bf16[128,256]{0,1:T(8,128)(2,1)S(1)} %pad_maximum_fusion.1), channel_id=1, source_target_pairs={{0,28},{4,32},{8,36},{12,40},{16,44},{20,48},{24,52},{28,56},{32,6... | collective-permute-start | bytes 196616 | tf_op jit(solution)/shard_map/ppermute | solution.py:15
  83.6 118.3 %collective-permute-start.10 = (bf16[128,256]{0,1:T(8,128)(2,1)S(1)}, bf16[128,256]{0,1:T(8,128)(2,1)S(1)}, u32[]{:S(2)}, u32[]{:S(2)}) collective-permute-start(bf16[128,256]{0,1:T(8,128)(2,1)S(1)} %pad_maximum_fusion.1), channel_id=1, source_target_pairs={{0,24},{4,28},{8,32},{12,36},{16,40},{20,44},{24,48},{28,52},{32,5... | collective-permute-start | bytes 196616 | tf_op jit(solution)/shard_map/ppermute | solution.py:15
  88.1 117.7 %collective-permute-start.11 = (bf16[128,256]{0,1:T(8,128)(2,1)S(1)}, bf16[128,256]{0,1:T(8,128)(2,1)S(1)}, u32[]{:S(2)}, u32[]{:S(2)}) collective-permute-start(bf16[128,256]{0,1:T(8,128)(2,1)S(1)} %pad_maximum_fusion.1), channel_id=1, source_target_pairs={{0,20},{4,24},{8,28},{12,32},{16,36},{20,40},{24,44},{28,48},{32,5... | collective-permute-start | bytes 196616 | tf_op jit(solution)/shard_map/ppermute | solution.py:15
  91.5 33.0 %collective-permute-start = (s32[128]{0:T(128)S(1)}, s32[128]{0:T(128)S(1)}, u32[]{:S(2)}, u32[]{:S(2)}) collective-permute-start(s32[128]{0:T(128)S(1)} %copy-done.4), channel_id=1, source_target_pairs={{0,32},{4,36},{8,40},{12,44},{16,48},{20,52},{24,56},{28,60},{32,6... | collective-permute-start | bytes 1544 | tf_op jit(solution)/shard_map/ppermute | solution.py:15
  113.2 113.9 %all-to-all-start = ((bf16[2,128,2048]{2,0,1:T(2,128)(2,1)}), bf16[2,128,2048]{2,0,1:T(2,128)(2,1)S(1)}, u32[]{:S(2)}, u32[]{:S(2)}) async-start(bf16[2,128,2048]{2,0,1:T(2,128)(2,1)} %pad_maximum_fusion), calls=%async_computation | async-start | bytes 2097152 | tf_op jit(solution)/shard_map/all_to_all | solution.py:136
  123.4 93.0 %all-gather.8.cloned.1.call-start = ((), (), s32[]{:S(2)}) async-start(), calls=%async_computation.3 | async-start | bytes 1585152 | tf_op jit(solution)/shard_map/all_gather | solution.py:110
  124.2 141.1 %reduce-scatter.4.cloned.1.call-start = ((), (), s32[]{:S(2)}) async-start(), calls=%async_computation.4 | async-start | bytes 491520
  124.5 17.1 %collective-permute-start.1 = (s32[128]{0:T(128)S(1)}, s32[128]{0:T(128)S(1)}, u32[]{:S(2)}, u32[]{:S(2)}) collective-permute-start(s32[128]{0:T(128)S(1)} %copy-done.4), channel_id=1, source_target_pairs={{0,28},{4,32},{8,36},{12,40},{16,44},{20,48},{24,52},{28,56},{32,6... | collective-permute-start | bytes 1544 | tf_op jit(solution)/shard_map/ppermute | solution.py:15
  141.6 9.2 %collective-permute-start.2 = (s32[128]{0:T(128)S(1)}, s32[128]{0:T(128)S(1)}, u32[]{:S(2)}, u32[]{:S(2)}) collective-permute-start(s32[128]{0:T(128)S(1)} %copy-done.4), channel_id=1, source_target_pairs={{0,24},{4,28},{8,32},{12,36},{16,40},{20,44},{24,48},{28,52},{32,5... | collective-permute-start | bytes 1544 | tf_op jit(solution)/shard_map/ppermute | solution.py:15
  150.8 9.5 %collective-permute-start.3 = (s32[128]{0:T(128)S(1)}, s32[128]{0:T(128)S(1)}, u32[]{:S(2)}, u32[]{:S(2)}) collective-permute-start(s32[128]{0:T(128)S(1)} %copy-done.4), channel_id=1, source_target_pairs={{0,20},{4,24},{8,28},{12,32},{16,36},{20,40},{24,44},{28,48},{32,5... | collective-permute-start | bytes 1544 | tf_op jit(solution)/shard_map/ppermute | solution.py:15
  160.2 6.3 %collective-permute-start.4 = (s32[128]{0:T(128)S(1)}, s32[128]{0:T(128)S(1)}, u32[]{:S(2)}, u32[]{:S(2)}) collective-permute-start(s32[128]{0:T(128)S(1)} %copy-done.4), channel_id=1, source_target_pairs={{0,16},{4,20},{8,24},{12,28},{16,32},{20,36},{24,40},{28,44},{32,4... | collective-permute-start | bytes 1544 | tf_op jit(solution)/shard_map/ppermute | solution.py:15
  166.5 7.5 %collective-permute-start.5 = (s32[128]{0:T(128)S(1)}, s32[128]{0:T(128)S(1)}, u32[]{:S(2)}, u32[]{:S(2)}) collective-permute-start(s32[128]{0:T(128)S(1)} %copy-done.4), channel_id=1, source_target_pairs={{0,12},{4,16},{8,20},{12,24},{16,28},{20,32},{24,36},{28,40},{32,4... | collective-permute-start | bytes 1544 | tf_op jit(solution)/shard_map/ppermute | solution.py:15
  174.0 4.1 %collective-permute-start.6 = (s32[128]{0:T(128)S(1)}, s32[128]{0:T(128)S(1)}, u32[]{:S(2)}, u32[]{:S(2)}) collective-permute-start(s32[128]{0:T(128)S(1)} %copy-done.4), channel_id=1, source_target_pairs={{0,8},{4,12},{8,16},{12,20},{16,24},{20,28},{24,32},{28,36},{32,40... | collective-permute-start | bytes 1544 | tf_op jit(solution)/shard_map/ppermute | solution.py:15
  178.1 5.4 %collective-permute-start.7 = (s32[128]{0:T(128)S(1)}, s32[128]{0:T(128)S(1)}, u32[]{:S(2)}, u32[]{:S(2)}) collective-permute-start(s32[128]{0:T(128)S(1)} %copy-done.4), channel_id=1, source_target_pairs={{0,4},{4,8},{8,12},{12,16},{16,20},{20,24},{24,28},{28,32},{32,36}... | collective-permute-start | bytes 1544 | tf_op jit(solution)/shard_map/ppermute | solution.py:15
  183.5 23.0 %collective-permute-start.12 = (bf16[128,256]{0,1:T(8,128)(2,1)S(1)}, bf16[128,256]{0,1:T(8,128)(2,1)S(1)}, u32[]{:S(2)}, u32[]{:S(2)}) collective-permute-start(bf16[128,256]{0,1:T(8,128)(2,1)S(1)} %pad_maximum_fusion.1), channel_id=1, source_target_pairs={{0,16},{4,20},{8,24},{12,28},{16,32},{20,36},{24,40},{28,44},{32,4... | collective-permute-start | bytes 196616 | tf_op jit(solution)/shard_map/ppermute | solution.py:15
  190.8 16.4 %collective-permute-start.13 = (bf16[128,256]{0,1:T(8,128)(2,1)S(1)}, bf16[128,256]{0,1:T(8,128)(2,1)S(1)}, u32[]{:S(2)}, u32[]{:S(2)}) collective-permute-start(bf16[128,256]{0,1:T(8,128)(2,1)S(1)} %pad_maximum_fusion.1), channel_id=1, source_target_pairs={{0,12},{4,16},{8,20},{12,24},{16,28},{20,32},{24,36},{28,40},{32,4... | collective-permute-start | bytes 196616 | tf_op jit(solution)/shard_map/ppermute | solution.py:15
  200.0 7.8 %collective-permute-start.14 = (bf16[128,256]{0,1:T(8,128)(2,1)S(1)}, bf16[128,256]{0,1:T(8,128)(2,1)S(1)}, u32[]{:S(2)}, u32[]{:S(2)}) collective-permute-start(bf16[128,256]{0,1:T(8,128)(2,1)S(1)} %pad_maximum_fusion.1), channel_id=1, source_target_pairs={{0,8},{4,12},{8,16},{12,20},{16,24},{20,28},{24,32},{28,36},{32,40... | collective-permute-start | bytes 196616 | tf_op jit(solution)/shard_map/ppermute | solution.py:15
  201.9 6.5 %collective-permute-start.15 = (bf16[128,256]{0,1:T(8,128)(2,1)S(1)}, bf16[128,256]{0,1:T(8,128)(2,1)S(1)}, u32[]{:S(2)}, u32[]{:S(2)}) collective-permute-start(bf16[128,256]{0,1:T(8,128)(2,1)S(1)} %pad_maximum_fusion.1), channel_id=1, source_target_pairs={{0,4},{4,8},{8,12},{12,16},{16,20},{20,24},{24,28},{28,32},{32,36}... | collective-permute-start | bytes 196616 | tf_op jit(solution)/shard_map/ppermute | solution.py:15
  221.4 1.5 copy-start.1
  227.0 0.7 copy-start.3
Sparse Core Ops, SparseCore 0:
  11.2 91.2 all-gather.5
  127.4 85.0 all-gather.7
  227.1 38.1 reduce-scatter.3
where the time goes:
time: 276 us; the launch traced here: 273 us
  starting transfers between devices  96.7 us (35%)
  blocking collectives  59.4 us (22%)
  waiting for transfers between devices  51.5 us (19%)
  local copies, waits for them, and re-layouts  22.6 us (8%)
  between operations  16.8 us (6%)
  other arithmetic  15.6 us (6%)
  matrix products  10.9 us (4%)
    ppermute x16, starting transfers between devices, shifted(): return lax.ppermute(block, axis, route)  86.4 us
    all_gather x1, blocking collectives, per_device(): keyval = add_rows(lax.all_gather(w_keyval, 'tok', axis=0, tiled=True))  59.4 us
    unnamed x4, waiting for transfers between devices  37.7 us
    ppermute x16, waiting for transfers between devices, shifted(): return lax.ppermute(block, axis, route)  13.8 us
    unnamed x32, local copies, waits for them, and re-layouts  13 us
    all_to_all x1, starting transfers between devices, per_device(): lax.all_to_all(jnp.stack(outgoing), 'tok', split_axis=1, concat_axis=1, t...  10.2 us
    gather x2, local copies, waits for them, and re-layouts, per_device(): fetched = jnp.take(pairs, jnp.clip(local_rows, 0, shard_rows - 1), axis=0)  7.88 us
  transfers between devices with their start and end apart: 20, of which 8 were waited for; matrix products, arithmetic and copies ran while one was open for 17% of the time, Pallas kernels for 0%

commit v1 on v0

v1 whole, which is shorter than its diff:
```python
import math

import jax
import jax.numpy as jnp
from jax import lax
from jax.sharding import Mesh, PartitionSpec as P

HD = 128
WINDOW = 1024
TOK = ("zh", "zl", "yh", "yl", "c")
PAD = 16
BF = jnp.bfloat16
F32 = jnp.float32


def ring(x, axes, step):
    size = lax.axis_size(axes)
    return lax.ppermute(x, axes, [(i, (i + step) % size) for i in range(size)])


def swap(x):
    return lax.ppermute(x, "c", [(0, 1), (1, 0)])


def earlier(x, distance):
    size = lax.axis_size(TOK)
    return lax.ppermute(x, TOK, [(i, i + distance) for i in range(size - distance)])


def gather_rows(chunk):
    near_y, near_z = ("yh", "yl"), ("zh", "zl")
    members = lax.axis_size(("zh", "yh"))
    half, quarter = members // 2, members // 4
    own = lax.all_to_all(
        jnp.broadcast_to(chunk[None], (members,) + chunk.shape), ("zh", "yh"), 0, 0, tiled=True
    )
    by_y = [ring(own[:half], near_y, 1), ring(own[half:], near_y, -1)]
    by_z = [ring(own[:half], near_z, 1), ring(own[half:], near_z, -1)]
    own_swapped = swap(own)
    diagonal = [
        ring(by_z[0][:quarter], near_y, 1),
        ring(by_z[0][quarter:], near_y, -1),
        ring(by_y[1][:quarter], near_z, 1),
        ring(by_y[1][quarter:], near_z, -1),
    ]
    sides = jnp.concatenate(by_y + by_z, axis=0)
    sides_swapped = swap(sides)
    corner = jnp.concatenate(diagonal, axis=0)
    corner_swapped = swap(corner)
    parts = [own, sides, corner, own_swapped, sides_swapped, corner_swapped]
    return jnp.concatenate(parts, axis=0).reshape(-1, chunk.shape[-1])


def gathered_index(devices, rows):
    zl, yl, core = lax.axis_index("zl"), lax.axis_index("yl"), lax.axis_index("c")
    n_yh = lax.axis_size("yh")
    per_class = lax.axis_size("zh") * n_yh
    place = jnp.arange(devices * PAD, dtype=jnp.int32)
    row = place % PAD
    member = (place // PAD) % per_class
    zh, yh = member // n_yh, member % n_yh
    group = (place // (PAD * per_class)) % 4
    other_z, other_y = group // 2, group % 2
    other_core = place // (PAD * per_class * 4)
    z = 2 * zh + (zl ^ other_z)
    y = 2 * yh + (yl ^ other_y)
    device = (z * (2 * n_yh) + y) * 2 + (core ^ other_core)
    return jnp.where(row < rows, device * rows + row, -1)


def per_device(tokens, norm_gain, w_query, w_keyval, w_out, segment_ids, lengths, member_prompt):
    shard_rows, width = tokens.shape
    q_cols = w_query.shape[1]
    kv_cols = w_keyval.shape[1]
    heads_here = q_cols // HD
    devices = lax.axis_size(TOK)
    n_head = lax.axis_size("head")
    tok_index = lax.axis_index(TOK)
    head_index = lax.axis_index("head")
    prompts = lengths.shape[0]
    w_rows = w_query.shape[0]

    chunk = jnp.concatenate([w_query, w_keyval, w_out.T], axis=1)
    chunk = jnp.pad(chunk, ((0, PAD - w_rows), (0, 0)))
    gathered = gather_rows(chunk)

    prompt_ends = jnp.cumsum(lengths)
    starts = prompt_ends - lengths
    global_index = tok_index * shard_rows + jnp.arange(shard_rows, dtype=jnp.int32)
    prompt_index = jnp.arange(prompts, dtype=jnp.int32)
    start_here = jnp.sum(
        jnp.where(segment_ids[:, None] == prompt_index[None, :], starts[None, :], 0), axis=1
    )
    positions = global_index - start_here
    frequency = 10000.0 ** (-(jnp.arange(HD // 2, dtype=F32) * 2.0 / HD))
    angles = positions.astype(F32)[:, None] * frequency[None, :]
    cosine, sine = jnp.cos(angles), jnp.sin(angles)
    cos_full = jnp.concatenate([cosine, cosine], axis=1)
    sin_full = jnp.concatenate([-sine, sine], axis=1)

    def rotate(values):
        swapped = jnp.concatenate([values[:, HD // 2 :], values[:, : HD // 2]], axis=1)
        return values * cos_full + swapped * sin_full

    widened = tokens.astype(F32)
    normed = (
        widened
        * lax.rsqrt(jnp.mean(widened * widened, axis=1, keepdims=True) + 1e-06)
        * norm_gain.astype(F32)
    ).astype(BF)
    order = gathered_index(devices, w_rows)
    placing = (jnp.arange(width, dtype=jnp.int32)[:, None] == order[None, :]).astype(BF)
    placed = jnp.dot(normed, placing, preferred_element_type=F32).astype(BF)
    projected = jnp.dot(placed, gathered[:, : q_cols + kv_cols], preferred_element_type=F32)
    keyval = projected[:, q_cols:]
    pairs = jnp.concatenate([rotate(keyval[:, :HD]), keyval[:, HD:]], axis=1).astype(BF)

    chip_reach = -(-WINDOW // (2 * shard_rows))
    behind = [earlier(pairs, 2 * k) for k in range(chip_reach, 0, -1)] + [pairs]
    own_keys = jnp.concatenate(behind, axis=0)
    other_keys = swap(own_keys)
    all_pairs = jnp.concatenate([own_keys, other_keys], axis=0)
    core = lax.axis_index("c")
    own_chip = tok_index // 2
    key_place = jnp.arange(2 * (chip_reach + 1) * shard_rows, dtype=jnp.int32)
    key_block = key_place // shard_rows
    key_chip = own_chip - chip_reach + key_block % (chip_reach + 1)
    key_core = core ^ (key_block // (chip_reach + 1))
    key_index = (2 * key_chip + key_core) * shard_rows + key_place % shard_rows

    queries = jnp.concatenate(
        [rotate(projected[:, s * HD : (s + 1) * HD]) for s in range(heads_here)], axis=0
    ).astype(BF)
    scores = lax.dot_general(
        queries, all_pairs[:, :HD], (((1,), (1,)), ((), ())), preferred_element_type=F32
    ) * (1.0 / math.sqrt(HD))
    allowed = (
        (key_index[None, :] >= start_here[:, None])
        & (key_index[None, :] <= global_index[:, None])
        & (key_index[None, :] > global_index[:, None] - WINDOW)
        & (key_index[None, :] >= 0)
    )
    scores = scores.reshape(heads_here, shard_rows, -1)
    scores = jnp.where(allowed[None], scores, -jnp.inf)
    largest = jnp.max(scores, axis=2, keepdims=True)
    weights = jnp.exp(scores - largest)
    total = jnp.sum(weights, axis=2, keepdims=True)
    probs = weights.astype(BF).reshape(heads_here * shard_rows, -1)
    summed = jnp.dot(probs, all_pairs[:, HD:], preferred_element_type=F32)
    attention = (summed / total.reshape(-1, 1)).astype(BF)
    attention = jnp.concatenate(
        [attention[s * shard_rows : (s + 1) * shard_rows] for s in range(heads_here)], axis=1
    )

    slots_here = WINDOW // devices
    col_share = kv_cols // n_head
    first_segment = jnp.sum((prompt_ends <= tok_index * shard_rows).astype(jnp.int32))
    slot_index = jnp.arange(WINDOW, dtype=jnp.int32)
    share = lax.dynamic_slice_in_dim(pairs, head_index * col_share, col_share, 1)
    pieces = []
    for local_seg in range(2):
        prompt_here = first_segment + local_seg
        matches = prompt_index == prompt_here
        prompt_size = jnp.sum(jnp.where(matches, lengths, 0))
        prompt_start = jnp.sum(jnp.where(matches, starts, 0))
        lowest = prompt_size - WINDOW
        places = lowest + jnp.mod(slot_index - lowest, WINDOW)
        local_rows = prompt_start + places - tok_index * shard_rows
        usable = (prompt_here < prompts) & (places >= 0)
        local_rows = jnp.where(usable, local_rows, -1)
        pick = (local_rows[:, None] == jnp.arange(shard_rows, dtype=jnp.int32)[None, :]).astype(BF)
        pieces.append(jnp.dot(pick, share, preferred_element_type=F32).astype(BF))
    outgoing = jnp.concatenate(pieces, axis=1).reshape(devices, slots_here, 2 * col_share)
    incoming = lax.all_to_all(outgoing, TOK, 0, 0, tiled=True)
    source_rows = jnp.arange(devices, dtype=jnp.int32) * shard_rows
    source_first = jnp.sum((prompt_ends[None, :] <= source_rows[:, None]).astype(jnp.int32), axis=1)
    table_rows = 32
    table_index = jnp.arange(table_rows, dtype=jnp.int32)
    table = jnp.zeros((table_rows, slots_here, col_share), F32)
    for local_seg in range(2):
        chooser = (source_first[None, :] + local_seg == table_index[:, None]).astype(BF)
        table = table + jnp.einsum(
            "ps,sjl->pjl",
            chooser,
            incoming[:, :, local_seg * col_share : (local_seg + 1) * col_share],
            preferred_element_type=F32,
        )
    table = table.astype(BF).reshape(shard_rows, -1)

    partial_out = lax.dot_general(
        attention, gathered[:, q_cols + kv_cols :], (((1,), (1,)), ((), ())), preferred_element_type=F32
    ).astype(BF)
    partial_out = lax.dot_general(
        partial_out, placing, (((1,), (1,)), ((), ())), preferred_element_type=F32
    ).astype(BF)
    quarter_cols = width // n_head
    sending = jnp.stack(
        [
            jnp.concatenate([partial_out[:, k * quarter_cols : (k + 1) * quarter_cols], table], axis=1)
            for k in range(n_head)
        ]
    )
    arrived = lax.all_to_all(sending, "head", 0, 0, tiled=True)
    residual = lax.dynamic_slice_in_dim(tokens, head_index * quarter_cols, quarter_cols, 1)
    mixed = (
        residual.astype(F32) + jnp.sum(arrived[:, :, :quarter_cols].astype(F32), axis=0)
    ).astype(BF)

    slot_table = arrived[:, :, quarter_cols:].reshape(n_head, table_rows, slots_here, col_share)
    member_pick = (member_prompt[:, None] == table_index[None, :]).astype(BF)
    cycle_cache = jnp.einsum("mp,hpjl->mjhl", member_pick, slot_table, preferred_element_type=F32)
    cycle_cache = cycle_cache.astype(BF).reshape(member_prompt.shape[0], slots_here, kv_cols)
    return (mixed, cycle_cache)


def solution(mesh):
    cut = Mesh(mesh.devices.reshape(4, 2, 4, 2, 2, 4), TOK + ("head",))
    return jax.shard_map(
        per_device,
        mesh=cut,
        in_specs=(
            P(TOK, None),
            P(),
            P(TOK, "head"),
            P(TOK, None),
            P("head", TOK),
            P(TOK),
            P(),
            P("head"),
        ),
        out_specs=(P(TOK, "head"), P("head", TOK, None)),
        check_vma=False,
    )
```

time: 276 us -> 151 us (0.55)
  blocking collectives: 59.4 us -> 0 us
  waiting for transfers between devices: 51.5 us -> 31.8 us
  local copies, waits for them, and re-layouts: 22.6 us -> 6.74 us
  between operations: 16.8 us -> 3.86 us
  starting transfers between devices: 96.7 us -> 84.2 us
  other arithmetic: 15.6 us -> 10.8 us
    all_gather x1 -> x0, blocking collectives: 59.4 us -> none  [per_device(): keyval = add_rows(lax.all_gather(w_keyval, 'tok', axis=0, tiled=True))]
    unnamed x4 -> x0, waiting for transfers between devices: 37.7 us -> none
    ppermute x16, starting transfers between devices: 86.4 us -> 51.7 us  [the longest x8 26 us: ring(): return lax.ppermute(x, axes, [(i, (i + step) % size) for i in range(size)])]
    all_to_all x1 -> x3, waiting for transfers between devices: 0.01 us -> 29.1 us  [the longest x1 11.5 us: gather_rows(): lax.all_to_all(jnp.broadcast_to(chunk[None], (members,) + chunk.shape), (...]
    all_to_all x1 -> x3, starting transfers between devices: 10.2 us -> 32.6 us  [the longest x1 16.2 us: gather_rows(): lax.all_to_all(jnp.broadcast_to(chunk[None], (members,) + chunk.shape), (...]
    ppermute x16, waiting for transfers between devices: 13.8 us -> 2.61 us  [the longest x4 1.32 us: earlier(): lax.ppermute(x, TOK, [(i, i + distance) for i in range(size - distance)])]
    unnamed x32 -> x22, local copies, waits for them, and re-layouts: 13 us -> 3.37 us
    gather x2 -> x0, local copies, waits for them, and re-layouts: 7.88 us -> none  [per_device(): fetched = jnp.take(pairs, jnp.clip(local_rows, 0, shard_rows - 1), axis=0)]
  transfers between devices with their start and end apart: 20 -> 19, of which waited for: 8 -> 6; matrix products, arithmetic and copies ran while one was open for 17% -> 11% of each run, Pallas kernels for 0% -> 0%
where the time goes in v1:
time: 151 us; the launch traced here: 150 us
  starting transfers between devices  84.2 us (56%)
  waiting for transfers between devices  31.8 us (21%)
  matrix products  12.2 us (8%)
  other arithmetic  10.8 us (7%)
  local copies, waits for them, and re-layouts  6.74 us (4%)
  between operations  3.86 us (3%)
    ppermute x8, starting transfers between devices, ring(): return lax.ppermute(x, axes, [(i, (i + step) % size) for i in range(size)])  26 us
    all_to_all x1, starting transfers between devices, gather_rows(): lax.all_to_all(jnp.broadcast_to(chunk[None], (members,) + chunk.shape), (...  16.2 us
    ppermute x4, starting transfers between devices, swap(): return lax.ppermute(x, 'c', [(0, 1), (1, 0)])  14.3 us
    all_to_all x1, starting transfers between devices, per_device(): incoming = lax.all_to_all(outgoing, TOK, 0, 0, tiled=True)  12.4 us
    all_to_all x1, waiting for transfers between devices, gather_rows(): lax.all_to_all(jnp.broadcast_to(chunk[None], (members,) + chunk.shape), (...  11.5 us
    ppermute x4, starting transfers between devices, earlier(): lax.ppermute(x, TOK, [(i, i + distance) for i in range(size - distance)])  11.4 us
    all_to_all x1, waiting for transfers between devices, per_device(): arrived = lax.all_to_all(sending, 'head', 0, 0, tiled=True)  8.92 us
    all_to_all x1, waiting for transfers between devices, per_device(): incoming = lax.all_to_all(outgoing, TOK, 0, 0, tiled=True)  8.71 us
  transfers between devices with their start and end apart: 19, of which 6 were waited for; matrix products, arithmetic and copies ran while one was open for 11% of the time, Pallas kernels for 0%

profile of v1, /device:TPU:1, one launch (start us, length us, event | category | flops | bytes accessed | tf_op | source)
XLA Modules:
  0.0 149.6 jit_solution(7650605131612494207)
XLA Ops:
  0.6 0.8 fusion.67
  1.4 0.9 broadcast_in_dim.46
  2.2 16.2 %all-to-all-start = ((bf16[16,16,1024]{2,1,0:T(8,128)(2,1)}), bf16[16,16,1024]{2,1,0:T(8,128)(2,1)S(1)}, u32[]{:S(2)}, u32[]{:S(2)}) async-start(bf16[16,16,1024]{2,1,0:T(8,128)(2,1)} %broadcast_in_dim.46), calls=%async_computation | async-start | bytes 1048576 | tf_op jit(solution)/shard_map/all_to_all | solution.py:34
  18.6 1.2 fusion.19
  19.7 0.8 copy.29
  20.7 0.6 fusion.148
  21.9 2.0 %fusion.144 = (s32[]{:T(128)}, s32[]{:T(128)}, s32[]{:T(128)}, s32[]{:T(128)}, s32[31]{0:T(128)S(1)}) fusion(s32[31]{0:T(128)} %param.14, s32[]{:T(128)} %fusion.148, s32[]{:T(128)S(6)} %add.363, s32[31]{0:T(128)S(1)} %reduce.2), kind=kLoop, calls=%fused_computation.248 | loop fusion | flops 337 | bytes 396 | tf_op jit(solution)/shard_map/reduce_sum | solution.py:164
  24.1 0.7 select_reduce_fusion
  24.8 0.3 fusion.69
  25.1 0.3 and_and_fusion
  25.4 11.5 %all-to-all-done = bf16[16,16,1024]{2,1,0:T(8,128)(2,1)S(1)} async-done(((bf16[16,16,1024]{2,1,0:T(8,128)(2,1)}), bf16[16,16,1024]{2,1,0:T(8,128)(2,1)S(1)}, u32[]{:S(2)}, u32[]{:S(2)}) %all-to-all-start) | async-done | bytes 524320 | tf_op jit(solution)/shard_map/all_to_all | solution.py:34
  37.0 3.3 %collective-permute-start.2 = (bf16[8,16,1024]{2,1,0:T(8,128)(2,1)S(1)}, bf16[8,16,1024]{2,1,0:T(8,128)(2,1)S(1)}, u32[]{:S(2)}, u32[]{:S(2)}) collective-permute-start(bf16[8,16,1024]{2,1,0:T(8,128)(2,1)S(1)} %get-tuple-element.16), channel_id=1, source_target_pairs={{0,64},{64,128},{128,192},{192,256},{256,320},{320,384},{384,448},... | collective-permute-start | bytes 786440 | tf_op jit(solution)/shard_map/ppermute | solution.py:18
  41.0 0.7 convert_element_type.74
  42.9 1.3 subtract_select_fusion
  44.2 1.9 %collective-permute-start = (bf16[8,16,1024]{2,1,0:T(8,128)(2,1)S(1)}, bf16[8,16,1024]{2,1,0:T(8,128)(2,1)S(1)}, u32[]{:S(2)}, u32[]{:S(2)}) collective-permute-start(bf16[8,16,1024]{2,1,0:T(8,128)(2,1)S(1)} %get-tuple-element.16), channel_id=1, source_target_pairs={{0,8},{8,16},{16,24},{24,32},{32,40},{40,48},{48,56},{56,0},{1,9},... | collective-permute-start | bytes 786440 | tf_op jit(solution)/shard_map/ppermute | solution.py:18
  46.1 4.6 %collective-permute-start.1 = (bf16[8,16,1024]{2,1,0:T(8,128)(2,1)S(1)}, bf16[8,16,1024]{2,1,0:T(8,128)(2,1)S(1)}, u32[]{:S(2)}, u32[]{:S(2)}) collective-permute-start(bf16[8,16,1024]{2,1,0:T(8,128)(2,1)S(1)} %get-tuple-element.15), channel_id=1, source_target_pairs={{0,56},{8,0},{16,8},{24,16},{32,24},{40,32},{48,40},{56,48},{1,57}... | collective-permute-start | bytes 786440 | tf_op jit(solution)/shard_map/ppermute | solution.py:18
  50.7 3.2 %collective-permute-start.3 = (bf16[8,16,1024]{2,1,0:T(8,128)(2,1)S(1)}, bf16[8,16,1024]{2,1,0:T(8,128)(2,1)S(1)}, u32[]{:S(2)}, u32[]{:S(2)}) collective-permute-start(bf16[8,16,1024]{2,1,0:T(8,128)(2,1)S(1)} %get-tuple-element.15), channel_id=1, source_target_pairs={{0,448},{64,0},{128,64},{192,128},{256,192},{320,256},{384,320},{4... | collective-permute-start | bytes 786440 | tf_op jit(solution)/shard_map/ppermute | solution.py:18
  54.0 2.6 %collective-permute-start.4 = (bf16[4,16,1024]{2,1,0:T(8,128)(2,1)S(1)}, bf16[4,16,1024]{2,1,0:T(8,128)(2,1)S(1)}, u32[]{:S(2)}, u32[]{:S(2)}) collective-permute-start(bf16[4,16,1024]{2,1,0:T(8,128)(2,1)S(1)} %get-tuple-element.37), channel_id=1, source_target_pairs={{0,8},{8,16},{16,24},{24,32},{32,40},{40,48},{48,56},{56,0},{1,9},... | collective-permute-start | bytes 393224 | tf_op jit(solution)/shard_map/ppermute | solution.py:18
  56.6 3.9 %collective-permute-start.5 = (bf16[4,16,1024]{2,1,0:T(8,128)(2,1)S(1)}, bf16[4,16,1024]{2,1,0:T(8,128)(2,1)S(1)}, u32[]{:S(2)}, u32[]{:S(2)}) collective-permute-start(bf16[4,16,1024]{2,1,0:T(8,128)(2,1)S(1)} %get-tuple-element.36), channel_id=1, source_target_pairs={{0,56},{8,0},{16,8},{24,16},{32,24},{40,32},{48,40},{56,48},{1,57}... | collective-permute-start | bytes 393224 | tf_op jit(solution)/shard_map/ppermute | solution.py:18
  60.5 2.1 %collective-permute-start.6 = (bf16[4,16,1024]{2,1,0:T(8,128)(2,1)S(1)}, bf16[4,16,1024]{2,1,0:T(8,128)(2,1)S(1)}, u32[]{:S(2)}, u32[]{:S(2)}) collective-permute-start(bf16[4,16,1024]{2,1,0:T(8,128)(2,1)S(1)} %get-tuple-element.35), channel_id=1, source_target_pairs={{0,64},{64,128},{128,192},{192,256},{256,320},{320,384},{384,448},... | collective-permute-start | bytes 393224 | tf_op jit(solution)/shard_map/ppermute | solution.py:18
  62.6 4.4 %collective-permute-start.7 = (bf16[4,16,1024]{2,1,0:T(8,128)(2,1)S(1)}, bf16[4,16,1024]{2,1,0:T(8,128)(2,1)S(1)}, u32[]{:S(2)}, u32[]{:S(2)}) collective-permute-start(bf16[4,16,1024]{2,1,0:T(8,128)(2,1)S(1)} %get-tuple-element.34), channel_id=1, source_target_pairs={{0,448},{64,0},{128,64},{192,128},{256,192},{320,256},{384,320},{4... | collective-permute-start | bytes 393224 | tf_op jit(solution)/shard_map/ppermute | solution.py:18
  67.2 6.7 %collective-permute-start.9 = (bf16[32,16,1024]{2,1,0:T(8,128)(2,1)S(1)}, bf16[32,16,1024]{2,1,0:T(8,128)(2,1)S(1)}, u32[]{:S(2)}, u32[]{:S(2)}) collective-permute-start(bf16[32,16,1024]{2,1,0:T(8,128)(2,1)S(1)} %pad_maximum_fusion), channel_id=1, source_target_pairs={{0,4},{4,0},{1,5},{5,1},{2,6},{6,2},{3,7},{7,3},{8,12},{12,8},{9,1... | collective-permute-start | bytes 3145736 | tf_op jit(solution)/shard_map/ppermute | solution.py:22
  74.0 1.9 %collective-permute-start.8 = (bf16[16,16,1024]{2,1,0:T(8,128)(2,1)S(1)}, bf16[16,16,1024]{2,1,0:T(8,128)(2,1)S(1)}, u32[]{:S(2)}, u32[]{:S(2)}) collective-permute-start(bf16[16,16,1024]{2,1,0:T(8,128)(2,1)S(1)} %all-to-all-done), channel_id=1, source_target_pairs={{0,4},{4,0},{1,5},{5,1},{2,6},{6,2},{3,7},{7,3},{8,12},{12,8},{9,1... | collective-permute-start | bytes 1572872 | tf_op jit(solution)/shard_map/ppermute | solution.py:22
  76.1 2.4 %collective-permute-start.10 = (bf16[16,16,1024]{2,1,0:T(8,128)(2,1)S(1)}, bf16[16,16,1024]{2,1,0:T(8,128)(2,1)S(1)}, u32[]{:S(2)}, u32[]{:S(2)}) collective-permute-start(bf16[16,16,1024]{2,1,0:T(8,128)(2,1)S(1)} %pad_maximum_fusion.1), channel_id=1, source_target_pairs={{0,4},{4,0},{1,5},{5,1},{2,6},{6,2},{3,7},{7,3},{8,12},{12,8},{9,1... | collective-permute-start | bytes 1572872 | tf_op jit(solution)/shard_map/ppermute | solution.py:22
  78.7 1.3 collective-permute-done.10
  80.0 1.9 %copy-done.1 = bf16[128,16,1024]{2,1,0:T(8,128)(2,1)} copy-done((bf16[128,16,1024]{2,1,0:T(8,128)(2,1)}, bf16[128,16,1024]{2,1,0:T(8,128)(2,1)S(1)}, u32[]{:S(2)}) %copy-start.1) | copy-done | bytes 4194328
  82.0 4.9 %fusion.5 = f32[128,640]{1,0:T(8,128)S(1)} fusion(bf16[2048,1024]{1,0:T(8,128)(2,1)} %bitcast.29, s32[2048]{0:T(1024)S(1)} %fusion.101, bf16[128,1536]{1,0:T(8,128)(2,1)S(1)} %copy-done, f32[1536]{0:T(1024)S(1)} %convert_element_type.74, f32[128]{0:T(128)S(1)} %add_rsqrt_fusion), kind=kOutput, calls=%fused_computation.7 | convolution fusion | flops 1145044992 | bytes 3357184 | tf_op jit(solution)/shard_map/dot_general | solution.py:114
  87.3 4.1 %collective-permute-start.11 = (bf16[128,256]{1,0:T(8,128)(2,1)S(1)}, bf16[128,256]{1,0:T(8,128)(2,1)S(1)}, u32[]{:S(2)}, u32[]{:S(2)}) collective-permute-start(bf16[128,256]{1,0:T(8,128)(2,1)S(1)} %pad_maximum_fusion.8), channel_id=1, source_target_pairs={{0,32},{4,36},{8,40},{12,44},{16,48},{20,52},{24,56},{28,60},{32,6... | collective-permute-start | bytes 196616 | tf_op jit(solution)/shard_map/ppermute | solution.py:27
  91.4 2.4 %collective-permute-start.12 = (bf16[128,256]{1,0:T(8,128)(2,1)S(1)}, bf16[128,256]{1,0:T(8,128)(2,1)S(1)}, u32[]{:S(2)}, u32[]{:S(2)}) collective-permute-start(bf16[128,256]{1,0:T(8,128)(2,1)S(1)} %pad_maximum_fusion.8), channel_id=1, source_target_pairs={{0,24},{4,28},{8,32},{12,36},{16,40},{20,44},{24,48},{28,52},{32,5... | collective-permute-start | bytes 196616 | tf_op jit(solution)/shard_map/ppermute | solution.py:27
  93.9 1.8 %collective-permute-start.13 = (bf16[128,256]{1,0:T(8,128)(2,1)S(1)}, bf16[128,256]{1,0:T(8,128)(2,1)S(1)}, u32[]{:S(2)}, u32[]{:S(2)}) collective-permute-start(bf16[128,256]{1,0:T(8,128)(2,1)S(1)} %pad_maximum_fusion.8), channel_id=1, source_target_pairs={{0,16},{4,20},{8,24},{12,28},{16,32},{20,36},{24,40},{28,44},{32,4... | collective-permute-start | bytes 196616 | tf_op jit(solution)/shard_map/ppermute | solution.py:27
  95.7 3.1 %collective-permute-start.14 = (bf16[128,256]{1,0:T(8,128)(2,1)S(1)}, bf16[128,256]{1,0:T(8,128)(2,1)S(1)}, u32[]{:S(2)}, u32[]{:S(2)}) collective-permute-start(bf16[128,256]{1,0:T(8,128)(2,1)S(1)} %pad_maximum_fusion.8), channel_id=1, source_target_pairs={{0,8},{4,12},{8,16},{12,20},{16,24},{20,28},{24,32},{28,36},{32,40... | collective-permute-start | bytes 196616 | tf_op jit(solution)/shard_map/ppermute | solution.py:27
  98.8 0.4 convolution_convert_fusion.3
  99.5 1.1 collective-permute-done.14
  100.6 3.2 %collective-permute-start.15 = (bf16[640,256]{1,0:T(8,128)(2,1)S(1)}, bf16[640,256]{1,0:T(8,128)(2,1)S(1)}, u32[]{:S(2)}, u32[]{:S(2)}) collective-permute-start(bf16[640,256]{1,0:T(8,128)(2,1)S(1)} %get-tuple-element.41), channel_id=1, source_target_pairs={{0,4},{4,0},{1,5},{5,1},{2,6},{6,2},{3,7},{7,3},{8,12},{12,8},{9,1... | collective-permute-start | bytes 983048 | tf_op jit(solution)/shard_map/ppermute | solution.py:22
  103.9 0.4 convolution_convert_fusion.2
  104.3 0.8 copy.30
  105.2 12.4 %all-to-all-start.1 = ((bf16[128,8,128]{2,1,0:T(8,128)(2,1)}), bf16[128,8,128]{2,1,0:T(8,128)(2,1)S(1)}, u32[]{:S(2)}, u32[]{:S(2)}) async-start(bf16[128,8,128]{2,1,0:T(8,128)(2,1)} %bitcast.5), calls=%async_computation.1 | async-start | bytes 524288 | tf_op jit(solution)/shard_map/all_to_all | solution.py:174
  117.7 0.6 fusion.161
  118.3 0.4 fusion.9
  118.7 0.5 fusion.13
  119.3 4.7 %fusion.8 = bf16[128,1536]{1,0:T(8,128)(2,1)S(1)} fusion(s32[2048]{0:T(1024)S(1)} %fusion.101, bf16[2048,1024]{1,0:T(8,128)(2,1)} %bitcast.30, bf16[128,128]{0,1:T(8,128)(2,1)S(1)} %get-tuple-element.39, bf16[128,128]{0,1:T(8,128)(2,1)S(1)} %get-tuple-element.40, bf16[128,128]{0,1:T(8,128)(2,1)S(1)} %get-tuple-element.38), kind=kOutput, calls=%fused_computation.10 | convolution fusion | flops 1010532352 | bytes 2072576 | tf_op jit(solution)/shard_map/dot_general | solution.py:193
  124.1 8.7 %all-to-all-done.1 = bf16[128,8,128]{2,1,0:T(8,128)(2,1)S(1)} async-done(((bf16[128,8,128]{2,1,0:T(8,128)(2,1)}), bf16[128,8,128]{2,1,0:T(8,128)(2,1)S(1)}, u32[]{:S(2)}, u32[]{:S(2)}) %all-to-all-start.1) | async-done | bytes 262176 | tf_op jit(solution)/shard_map/all_to_all | solution.py:174
  133.4 0.9 pad_maximum_fusion.2
  134.3 4.0 %all-to-all-start.2 = ((bf16[4,128,512]{2,1,0:T(8,128)(2,1)}), bf16[4,128,512]{2,1,0:T(8,128)(2,1)S(1)}, u32[]{:S(2)}, u32[]{:S(2)}) async-start(bf16[4,128,512]{2,1,0:T(8,128)(2,1)} %pad_maximum_fusion.2), calls=%async_computation.2 | async-start | bytes 1048576 | tf_op jit(solution)/shard_map/all_to_all | solution.py:203
  138.3 8.9 %all-to-all-done.2 = bf16[4,128,512]{2,1,0:T(8,128)(2,1)S(1)} async-done(((bf16[4,128,512]{2,1,0:T(8,128)(2,1)}), bf16[4,128,512]{2,1,0:T(8,128)(2,1)S(1)}, u32[]{:S(2)}, u32[]{:S(2)}) %all-to-all-start.2) | async-done | bytes 524320 | tf_op jit(solution)/shard_map/all_to_all | solution.py:203
  147.4 0.3 fusion.12
  147.8 1.1 copy.36
  148.9 0.7 add_convert_fusion
  (73 shorter events, 2.8 us)
Async XLA Ops:
  2.2 34.7 %all-to-all-start = ((bf16[16,16,1024]{2,1,0:T(8,128)(2,1)}), bf16[16,16,1024]{2,1,0:T(8,128)(2,1)S(1)}, u32[]{:S(2)}, u32[]{:S(2)}) async-start(bf16[16,16,1024]{2,1,0:T(8,128)(2,1)} %broadcast_in_dim.46), calls=%async_computation | async-start | bytes 1048576 | tf_op jit(solution)/shard_map/all_to_all | solution.py:34
  37.0 16.9 %collective-permute-start.2 = (bf16[8,16,1024]{2,1,0:T(8,128)(2,1)S(1)}, bf16[8,16,1024]{2,1,0:T(8,128)(2,1)S(1)}, u32[]{:S(2)}, u32[]{:S(2)}) collective-permute-start(bf16[8,16,1024]{2,1,0:T(8,128)(2,1)S(1)} %get-tuple-element.16), channel_id=1, source_target_pairs={{0,64},{64,128},{128,192},{192,256},{256,320},{320,384},{384,448},... | collective-permute-start | bytes 786440 | tf_op jit(solution)/shard_map/ppermute | solution.py:18
  44.2 18.4 %collective-permute-start = (bf16[8,16,1024]{2,1,0:T(8,128)(2,1)S(1)}, bf16[8,16,1024]{2,1,0:T(8,128)(2,1)S(1)}, u32[]{:S(2)}, u32[]{:S(2)}) collective-permute-start(bf16[8,16,1024]{2,1,0:T(8,128)(2,1)S(1)} %get-tuple-element.16), channel_id=1, source_target_pairs={{0,8},{8,16},{16,24},{24,32},{32,40},{40,48},{48,56},{56,0},{1,9},... | collective-permute-start | bytes 786440 | tf_op jit(solution)/shard_map/ppermute | solution.py:18
  46.1 14.4 %collective-permute-start.1 = (bf16[8,16,1024]{2,1,0:T(8,128)(2,1)S(1)}, bf16[8,16,1024]{2,1,0:T(8,128)(2,1)S(1)}, u32[]{:S(2)}, u32[]{:S(2)}) collective-permute-start(bf16[8,16,1024]{2,1,0:T(8,128)(2,1)S(1)} %get-tuple-element.15), channel_id=1, source_target_pairs={{0,56},{8,0},{16,8},{24,16},{32,24},{40,32},{48,40},{56,48},{1,57}... | collective-permute-start | bytes 786440 | tf_op jit(solution)/shard_map/ppermute | solution.py:18
  50.7 16.3 %collective-permute-start.3 = (bf16[8,16,1024]{2,1,0:T(8,128)(2,1)S(1)}, bf16[8,16,1024]{2,1,0:T(8,128)(2,1)S(1)}, u32[]{:S(2)}, u32[]{:S(2)}) collective-permute-start(bf16[8,16,1024]{2,1,0:T(8,128)(2,1)S(1)} %get-tuple-element.15), channel_id=1, source_target_pairs={{0,448},{64,0},{128,64},{192,128},{256,192},{320,256},{384,320},{4... | collective-permute-start | bytes 786440 | tf_op jit(solution)/shard_map/ppermute | solution.py:18
  54.0 20.1 %collective-permute-start.4 = (bf16[4,16,1024]{2,1,0:T(8,128)(2,1)S(1)}, bf16[4,16,1024]{2,1,0:T(8,128)(2,1)S(1)}, u32[]{:S(2)}, u32[]{:S(2)}) collective-permute-start(bf16[4,16,1024]{2,1,0:T(8,128)(2,1)S(1)} %get-tuple-element.37), channel_id=1, source_target_pairs={{0,8},{8,16},{16,24},{24,32},{32,40},{40,48},{48,56},{56,0},{1,9},... | collective-permute-start | bytes 393224 | tf_op jit(solution)/shard_map/ppermute | solution.py:18
  56.6 19.4 %collective-permute-start.5 = (bf16[4,16,1024]{2,1,0:T(8,128)(2,1)S(1)}, bf16[4,16,1024]{2,1,0:T(8,128)(2,1)S(1)}, u32[]{:S(2)}, u32[]{:S(2)}) collective-permute-start(bf16[4,16,1024]{2,1,0:T(8,128)(2,1)S(1)} %get-tuple-element.36), channel_id=1, source_target_pairs={{0,56},{8,0},{16,8},{24,16},{32,24},{40,32},{48,40},{56,48},{1,57}... | collective-permute-start | bytes 393224 | tf_op jit(solution)/shard_map/ppermute | solution.py:18
  60.5 15.5 %collective-permute-start.6 = (bf16[4,16,1024]{2,1,0:T(8,128)(2,1)S(1)}, bf16[4,16,1024]{2,1,0:T(8,128)(2,1)S(1)}, u32[]{:S(2)}, u32[]{:S(2)}) collective-permute-start(bf16[4,16,1024]{2,1,0:T(8,128)(2,1)S(1)} %get-tuple-element.35), channel_id=1, source_target_pairs={{0,64},{64,128},{128,192},{192,256},{256,320},{320,384},{384,448},... | collective-permute-start | bytes 393224 | tf_op jit(solution)/shard_map/ppermute | solution.py:18
  62.6 13.3 %collective-permute-start.7 = (bf16[4,16,1024]{2,1,0:T(8,128)(2,1)S(1)}, bf16[4,16,1024]{2,1,0:T(8,128)(2,1)S(1)}, u32[]{:S(2)}, u32[]{:S(2)}) collective-permute-start(bf16[4,16,1024]{2,1,0:T(8,128)(2,1)S(1)} %get-tuple-element.34), channel_id=1, source_target_pairs={{0,448},{64,0},{128,64},{192,128},{256,192},{320,256},{384,320},{4... | collective-permute-start | bytes 393224 | tf_op jit(solution)/shard_map/ppermute | solution.py:18
  67.2 14.8 %copy-start = (bf16[128,1536]{1,0:T(8,128)(2,1)S(1)}, bf16[128,1536]{1,0:T(8,128)(2,1)}, u32[]{:S(2)}) copy-start(bf16[128,1536]{1,0:T(8,128)(2,1)} %param.8) | copy-start | bytes 1179652
  67.2 11.4 %collective-permute-start.9 = (bf16[32,16,1024]{2,1,0:T(8,128)(2,1)S(1)}, bf16[32,16,1024]{2,1,0:T(8,128)(2,1)S(1)}, u32[]{:S(2)}, u32[]{:S(2)}) collective-permute-start(bf16[32,16,1024]{2,1,0:T(8,128)(2,1)S(1)} %pad_maximum_fusion), channel_id=1, source_target_pairs={{0,4},{4,0},{1,5},{5,1},{2,6},{6,2},{3,7},{7,3},{8,12},{12,8},{9,1... | collective-permute-start | bytes 3145736 | tf_op jit(solution)/shard_map/ppermute | solution.py:22
  74.0 4.5 %collective-permute-start.8 = (bf16[16,16,1024]{2,1,0:T(8,128)(2,1)S(1)}, bf16[16,16,1024]{2,1,0:T(8,128)(2,1)S(1)}, u32[]{:S(2)}, u32[]{:S(2)}) collective-permute-start(bf16[16,16,1024]{2,1,0:T(8,128)(2,1)S(1)} %all-to-all-done), channel_id=1, source_target_pairs={{0,4},{4,0},{1,5},{5,1},{2,6},{6,2},{3,7},{7,3},{8,12},{12,8},{9,1... | collective-permute-start | bytes 1572872 | tf_op jit(solution)/shard_map/ppermute | solution.py:22
  76.1 3.9 %collective-permute-start.10 = (bf16[16,16,1024]{2,1,0:T(8,128)(2,1)S(1)}, bf16[16,16,1024]{2,1,0:T(8,128)(2,1)S(1)}, u32[]{:S(2)}, u32[]{:S(2)}) collective-permute-start(bf16[16,16,1024]{2,1,0:T(8,128)(2,1)S(1)} %pad_maximum_fusion.1), channel_id=1, source_target_pairs={{0,4},{4,0},{1,5},{5,1},{2,6},{6,2},{3,7},{7,3},{8,12},{12,8},{9,1... | collective-permute-start | bytes 1572872 | tf_op jit(solution)/shard_map/ppermute | solution.py:22
  80.0 1.9 %copy-start.1 = (bf16[128,16,1024]{2,1,0:T(8,128)(2,1)}, bf16[128,16,1024]{2,1,0:T(8,128)(2,1)S(1)}, u32[]{:S(2)}) copy-start(bf16[128,16,1024]{2,1,0:T(8,128)(2,1)S(1)} %constant_dynamic-update-slice_fusion) | copy-start | bytes 12582916
  87.3 11.9 %collective-permute-start.11 = (bf16[128,256]{1,0:T(8,128)(2,1)S(1)}, bf16[128,256]{1,0:T(8,128)(2,1)S(1)}, u32[]{:S(2)}, u32[]{:S(2)}) collective-permute-start(bf16[128,256]{1,0:T(8,128)(2,1)S(1)} %pad_maximum_fusion.8), channel_id=1, source_target_pairs={{0,32},{4,36},{8,40},{12,44},{16,48},{20,52},{24,56},{28,60},{32,6... | collective-permute-start | bytes 196616 | tf_op jit(solution)/shard_map/ppermute | solution.py:27
  91.4 7.8 %collective-permute-start.12 = (bf16[128,256]{1,0:T(8,128)(2,1)S(1)}, bf16[128,256]{1,0:T(8,128)(2,1)S(1)}, u32[]{:S(2)}, u32[]{:S(2)}) collective-permute-start(bf16[128,256]{1,0:T(8,128)(2,1)S(1)} %pad_maximum_fusion.8), channel_id=1, source_target_pairs={{0,24},{4,28},{8,32},{12,36},{16,40},{20,44},{24,48},{28,52},{32,5... | collective-permute-start | bytes 196616 | tf_op jit(solution)/shard_map/ppermute | solution.py:27
  93.9 5.6 %collective-permute-start.13 = (bf16[128,256]{1,0:T(8,128)(2,1)S(1)}, bf16[128,256]{1,0:T(8,128)(2,1)S(1)}, u32[]{:S(2)}, u32[]{:S(2)}) collective-permute-start(bf16[128,256]{1,0:T(8,128)(2,1)S(1)} %pad_maximum_fusion.8), channel_id=1, source_target_pairs={{0,16},{4,20},{8,24},{12,28},{16,32},{20,36},{24,40},{28,44},{32,4... | collective-permute-start | bytes 196616 | tf_op jit(solution)/shard_map/ppermute | solution.py:27
  95.7 4.9 %collective-permute-start.14 = (bf16[128,256]{1,0:T(8,128)(2,1)S(1)}, bf16[128,256]{1,0:T(8,128)(2,1)S(1)}, u32[]{:S(2)}, u32[]{:S(2)}) collective-permute-start(bf16[128,256]{1,0:T(8,128)(2,1)S(1)} %pad_maximum_fusion.8), channel_id=1, source_target_pairs={{0,8},{4,12},{8,16},{12,20},{16,24},{20,28},{24,32},{28,36},{32,40... | collective-permute-start | bytes 196616 | tf_op jit(solution)/shard_map/ppermute | solution.py:27
  100.6 16.9 %collective-permute-start.15 = (bf16[640,256]{1,0:T(8,128)(2,1)S(1)}, bf16[640,256]{1,0:T(8,128)(2,1)S(1)}, u32[]{:S(2)}, u32[]{:S(2)}) collective-permute-start(bf16[640,256]{1,0:T(8,128)(2,1)S(1)} %get-tuple-element.41), channel_id=1, source_target_pairs={{0,4},{4,0},{1,5},{5,1},{2,6},{6,2},{3,7},{7,3},{8,12},{12,8},{9,1... | collective-permute-start | bytes 983048 | tf_op jit(solution)/shard_map/ppermute | solution.py:22
  105.2 27.6 %all-to-all-start.1 = ((bf16[128,8,128]{2,1,0:T(8,128)(2,1)}), bf16[128,8,128]{2,1,0:T(8,128)(2,1)S(1)}, u32[]{:S(2)}, u32[]{:S(2)}) async-start(bf16[128,8,128]{2,1,0:T(8,128)(2,1)} %bitcast.5), calls=%async_computation.1 | async-start | bytes 524288 | tf_op jit(solution)/shard_map/all_to_all | solution.py:174
  124.0 23.4 %copy-start.2 = (s32[96]{0:T(128)S(1)}, s32[96]{0:T(128)}, u32[]{:S(2)}) copy-start(s32[96]{0:T(128)} %param.15) | copy-start | bytes 1156
  134.3 12.9 %all-to-all-start.2 = ((bf16[4,128,512]{2,1,0:T(8,128)(2,1)}), bf16[4,128,512]{2,1,0:T(8,128)(2,1)S(1)}, u32[]{:S(2)}, u32[]{:S(2)}) async-start(bf16[4,128,512]{2,1,0:T(8,128)(2,1)} %pad_maximum_fusion.2), calls=%async_computation.2 | async-start | bytes 1048576 | tf_op jit(solution)/shard_map/all_to_all | solution.py:203

commit v2 on v1

--- a/solution.py
+++ b/solution.py
@@ -5,10 +5,10 @@
 from jax import lax
 from jax.sharding import Mesh, PartitionSpec as P
 
+
 HD = 128
 WINDOW = 1024
 TOK = ("zh", "zl", "yh", "yl", "c")
-PAD = 16
 BF = jnp.bfloat16
 F32 = jnp.float32
 
@@ -28,47 +28,37 @@
 
 
 def gather_rows(chunk):
-    near_y, near_z = ("yh", "yl"), ("zh", "zl")
-    members = lax.axis_size(("zh", "yh"))
-    half, quarter = members // 2, members // 4
+    line = ("zh", "zl", "yh")
+    members = lax.axis_size(line)
+    n_zh = lax.axis_size("zh")
+    half = members // 2
     own = lax.all_to_all(
-        jnp.broadcast_to(chunk[None], (members,) + chunk.shape), ("zh", "yh"), 0, 0, tiled=True
-    )
-    by_y = [ring(own[:half], near_y, 1), ring(own[half:], near_y, -1)]
-    by_z = [ring(own[:half], near_z, 1), ring(own[half:], near_z, -1)]
+        jnp.broadcast_to(chunk[None], (members,) + chunk.shape), line, 0, 0, tiled=True
+    )
+    below = ring(own[:half], ("yh", "yl"), 1)
+    above = ring(own[half:], ("yh", "yl"), -1)
     own_swapped = swap(own)
-    diagonal = [
-        ring(by_z[0][:quarter], near_y, 1),
-        ring(by_z[0][quarter:], near_y, -1),
-        ring(by_y[1][:quarter], near_z, 1),
-        ring(by_y[1][quarter:], near_z, -1),
-    ]
-    sides = jnp.concatenate(by_y + by_z, axis=0)
+    sides = jnp.concatenate([below, above], axis=0)
     sides_swapped = swap(sides)
-    corner = jnp.concatenate(diagonal, axis=0)
-    corner_swapped = swap(corner)
-    parts = [own, sides, corner, own_swapped, sides_swapped, corner_swapped]
-    return jnp.concatenate(parts, axis=0).reshape(-1, chunk.shape[-1])
-
-
-def gathered_index(devices, rows):
-    zl, yl, core = lax.axis_index("zl"), lax.axis_index("yl"), lax.axis_index("c")
-    n_yh = lax.axis_size("yh")
-    per_class = lax.axis_size("zh") * n_yh
-    place = jnp.arange(devices * PAD, dtype=jnp.int32)
-    row = place % PAD
-    member = (place // PAD) % per_class
-    zh, yh = member // n_yh, member % n_yh
-    group = (place // (PAD * per_class)) % 4
-    other_z, other_y = group // 2, group % 2
-    other_core = place // (PAD * per_class * 4)
-    z = 2 * zh + (zl ^ other_z)
-    y = 2 * yh + (yl ^ other_y)
-    device = (z * (2 * n_yh) + y) * 2 + (core ^ other_core)
-    return jnp.where(row < rows, device * rows + row, -1)
-
-
-def per_device(tokens, norm_gain, w_query, w_keyval, w_out, segment_ids, lengths, member_prompt):
+    shape = (n_zh, members // n_zh) + chunk.shape
+    pieces = [piece.reshape(shape) for piece in (own, sides, own_swapped, sides_swapped)]
+    return jnp.stack(pieces, axis=1)
+
+
+def block_places(rows, offset, stacked):
+    yl, core = lax.axis_index("yl"), lax.axis_index("c")
+    n_zl, n_yh = lax.axis_size("zl"), lax.axis_size("yh")
+    place = jnp.arange(4 * n_zl * n_yh * stacked, dtype=jnp.int32)
+    row = place % stacked - offset
+    yh = (place // stacked) % n_yh
+    zl = (place // (stacked * n_yh)) % n_zl
+    piece = place // (stacked * n_yh * n_zl)
+    y = 2 * yh + (yl ^ (piece % 2))
+    device = (zl * (2 * n_yh) + y) * 2 + (core ^ (piece // 2))
+    return jnp.where((row >= 0) & (row < rows), device * rows + row, -1)
+
+
+def layer(tokens, norm_gain, w_query, w_keyval, w_out, segment_ids, lengths, member_prompt):
     shard_rows, width = tokens.shape
     q_cols = w_query.shape[1]
     kv_cols = w_keyval.shape[1]
@@ -80,9 +70,11 @@
     prompts = lengths.shape[0]
     w_rows = w_query.shape[0]
 
-    chunk = jnp.concatenate([w_query, w_keyval, w_out.T], axis=1)
-    chunk = jnp.pad(chunk, ((0, PAD - w_rows), (0, 0)))
-    gathered = gather_rows(chunk)
+    upper = jnp.concatenate([w_query, w_keyval[:, :HD]], axis=1)
+    lower = jnp.concatenate([w_keyval[:, HD:], w_out.T], axis=1)
+    chunk = jnp.concatenate([upper, lower], axis=0)
+    blocks = lax.axis_size("zh")
+    gathered = gather_rows(chunk).reshape(-1, chunk.shape[1])
 
     prompt_ends = jnp.cumsum(lengths)
     starts = prompt_ends - lengths
@@ -108,12 +100,58 @@
         * lax.rsqrt(jnp.mean(widened * widened, axis=1, keepdims=True) + 1e-06)
         * norm_gain.astype(F32)
     ).astype(BF)
-    order = gathered_index(devices, w_rows)
-    placing = (jnp.arange(width, dtype=jnp.int32)[:, None] == order[None, :]).astype(BF)
-    placed = jnp.dot(normed, placing, preferred_element_type=F32).astype(BF)
-    projected = jnp.dot(placed, gathered[:, : q_cols + kv_cols], preferred_element_type=F32)
-    keyval = projected[:, q_cols:]
-    pairs = jnp.concatenate([rotate(keyval[:, :HD]), keyval[:, HD:]], axis=1).astype(BF)
+    block_width = width // blocks
+    block_row = jnp.arange(block_width, dtype=jnp.int32)
+    upper_places = block_places(w_rows, 0, 2 * w_rows)
+    lower_places = block_places(w_rows, w_rows, 2 * w_rows)
+    upper_pick = (block_row[:, None] == upper_places[None, :]).astype(BF)
+    lower_pick = (block_row[:, None] == lower_places[None, :]).astype(BF)
+
+    def place(pick):
+        return jnp.concatenate(
+            [
+                jnp.dot(
+                    normed[:, k * block_width : (k + 1) * block_width],
+                    pick,
+                    preferred_element_type=F32,
+                ).astype(BF)
+                for k in range(blocks)
+            ],
+            axis=1,
+        )
+
+    placed_upper, placed_lower, lower_pick = lax.optimization_barrier(
+        (place(upper_pick), place(lower_pick), lower_pick)
+    )
+    projected = jnp.dot(placed_upper, gathered, preferred_element_type=F32)
+    values = jnp.dot(placed_lower, gathered[:, :HD], preferred_element_type=F32)
+    pairs = jnp.concatenate([rotate(projected[:, q_cols:]), values], axis=1).astype(BF)
+
+    slots_here = WINDOW // devices
+    col_share = kv_cols // n_head
+    first_segment = jnp.sum((prompt_ends <= tok_index * shard_rows).astype(jnp.int32))
+    slot_index = jnp.arange(WINDOW, dtype=jnp.int32)
+    share = lax.dynamic_slice_in_dim(pairs, head_index * col_share, col_share, 1)
+    picks = []
+    for local_seg in range(2):
+        prompt_here = first_segment + local_seg
+        matches = prompt_index == prompt_here
+        prompt_size = jnp.sum(jnp.where(matches, lengths, 0))
+        prompt_start = jnp.sum(jnp.where(matches, starts, 0))
+        lowest = prompt_size - WINDOW
+        places = lowest + jnp.mod(slot_index - lowest, WINDOW)
+        local_rows = prompt_start + places - tok_index * shard_rows
+        usable = (prompt_here < prompts) & (places >= 0)
+        local_rows = jnp.where(usable, local_rows, -1)
+        picks.append(local_rows[:, None] == jnp.arange(shard_rows, dtype=jnp.int32)[None, :])
+    pick = jnp.concatenate(picks, axis=1).astype(BF)
+    blank = jnp.zeros_like(share)
+    shares = jnp.concatenate(
+        [jnp.concatenate([share, blank], axis=1), jnp.concatenate([blank, share], axis=1)], axis=0
+    )
+    outgoing = jnp.dot(pick, shares, preferred_element_type=F32).astype(BF)
+    outgoing = outgoing.reshape(devices, slots_here, 2 * col_share)
+    incoming = lax.all_to_all(outgoing, TOK, 0, 0, tiled=True)
 
     chip_reach = -(-WINDOW // (2 * shard_rows))
     behind = [earlier(pairs, 2 * k) for k in range(chip_reach, 0, -1)] + [pairs]
@@ -152,26 +190,6 @@
         [attention[s * shard_rows : (s + 1) * shard_rows] for s in range(heads_here)], axis=1
     )
 
-    slots_here = WINDOW // devices
-    col_share = kv_cols // n_head
-    first_segment = jnp.sum((prompt_ends <= tok_index * shard_rows).astype(jnp.int32))
-    slot_index = jnp.arange(WINDOW, dtype=jnp.int32)
-    share = lax.dynamic_slice_in_dim(pairs, head_index * col_share, col_share, 1)
-    pieces = []
-    for local_seg in range(2):
-        prompt_here = first_segment + local_seg
-        matches = prompt_index == prompt_here
-        prompt_size = jnp.sum(jnp.where(matches, lengths, 0))
-        prompt_start = jnp.sum(jnp.where(matches, starts, 0))
-        lowest = prompt_size - WINDOW
-        places = lowest + jnp.mod(slot_index - lowest, WINDOW)
-        local_rows = prompt_start + places - tok_index * shard_rows
-        usable = (prompt_here < prompts) & (places >= 0)
-        local_rows = jnp.where(usable, local_rows, -1)
-        pick = (local_rows[:, None] == jnp.arange(shard_rows, dtype=jnp.int32)[None, :]).astype(BF)
-        pieces.append(jnp.dot(pick, share, preferred_element_type=F32).astype(BF))
-    outgoing = jnp.concatenate(pieces, axis=1).reshape(devices, slots_here, 2 * col_share)
-    incoming = lax.all_to_all(outgoing, TOK, 0, 0, tiled=True)
     source_rows = jnp.arange(devices, dtype=jnp.int32) * shard_rows
     source_first = jnp.sum((prompt_ends[None, :] <= source_rows[:, None]).astype(jnp.int32), axis=1)
     table_rows = 32
@@ -188,11 +206,21 @@
     table = table.astype(BF).reshape(shard_rows, -1)
 
     partial_out = lax.dot_general(
-        attention, gathered[:, q_cols + kv_cols :], (((1,), (1,)), ((), ())), preferred_element_type=F32
-    ).astype(BF)
-    partial_out = lax.dot_general(
-        partial_out, placing, (((1,), (1,)), ((), ())), preferred_element_type=F32
-    ).astype(BF)
+        attention, gathered[:, HD:], (((1,), (1,)), ((), ())), preferred_element_type=F32
+    ).astype(BF)
+    block_places_width = partial_out.shape[1] // blocks
+    partial_out = jnp.concatenate(
+        [
+            lax.dot_general(
+                partial_out[:, k * block_places_width : (k + 1) * block_places_width],
+                lower_pick,
+                (((1,), (1,)), ((), ())),
+                preferred_element_type=F32,
+            ).astype(BF)
+            for k in range(blocks)
+        ],
+        axis=1,
+    )
     quarter_cols = width // n_head
     sending = jnp.stack(
         [
@@ -216,7 +244,7 @@
 def solution(mesh):
     cut = Mesh(mesh.devices.reshape(4, 2, 4, 2, 2, 4), TOK + ("head",))
     return jax.shard_map(
-        per_device,
+        layer,
         mesh=cut,
         in_specs=(
             P(TOK, None),

time: 151 us -> 135 us (0.89)
  starting transfers between devices: 84.2 us -> 65.6 us
  waiting for transfers between devices: 31.8 us -> 37.5 us
  matrix products: 12.2 us -> 9.39 us
    ppermute x8 -> x2, starting transfers between devices: 26 us -> 6.48 us  [ring(): return lax.ppermute(x, axes, [(i, (i + step) % size) for i in range(size)])]
    ppermute x4, starting transfers between devices: 11.4 us -> 15.5 us  [earlier(): lax.ppermute(x, TOK, [(i, i + distance) for i in range(size - distance)])]
    dot_general x9 -> x21, matrix products: 12.2 us -> 9.39 us  [the longest x8 3.39 us: place(): jnp.dot(normed[:, k * block_width:(k + 1) * block_width], pick, preferred...]
    reduce_sum x7, other arithmetic: 5.14 us -> 2.8 us  [the longest x1 1.35 us: layer(): prompt_size = jnp.sum(jnp.where(matches, lengths, 0))]
    all_to_all x3, waiting for transfers between devices: 29.1 us -> 31.4 us  [the longest x1 12.1 us: gather_rows(): lax.all_to_all(jnp.broadcast_to(chunk[None], (members,) + chunk.shape), l...]
    ppermute x8 -> x2, waiting for transfers between devices: 0.02 us -> 1.98 us  [ring(): return lax.ppermute(x, axes, [(i, (i + step) % size) for i in range(size)])]
    all_to_all x3, starting transfers between devices: 32.6 us -> 30.9 us  [the longest x1 16.5 us: gather_rows(): lax.all_to_all(jnp.broadcast_to(chunk[None], (members,) + chunk.shape), l...]
    ppermute x4 -> x3, starting transfers between devices: 14.3 us -> 12.7 us  [swap(): return lax.ppermute(x, 'c', [(0, 1), (1, 0)])]
  transfers between devices with their start and end apart: 19 -> 12, of which waited for: 6 -> 6; matrix products, arithmetic and copies ran while one was open for 11% -> 13% of each run, Pallas kernels for 0% -> 0%
where the time goes in v2:
time: 135 us
  starting transfers between devices  65.6 us (49%)
  waiting for transfers between devices  37.5 us (28%)
  other arithmetic  9.92 us (7%)
  matrix products  9.39 us (7%)
  local copies, waits for them, and re-layouts  8.18 us (6%)
  between operations  3.95 us (3%)
    all_to_all x1, starting transfers between devices, gather_rows(): lax.all_to_all(jnp.broadcast_to(chunk[None], (members,) + chunk.shape), l...  16.5 us
    ppermute x4, starting transfers between devices, earlier(): lax.ppermute(x, TOK, [(i, i + distance) for i in range(size - distance)])  15.5 us
    ppermute x3, starting transfers between devices, swap(): return lax.ppermute(x, 'c', [(0, 1), (1, 0)])  12.7 us
    all_to_all x1, waiting for transfers between devices, gather_rows(): lax.all_to_all(jnp.broadcast_to(chunk[None], (members,) + chunk.shape), l...  12.1 us
    all_to_all x1, waiting for transfers between devices, layer(): incoming = lax.all_to_all(outgoing, TOK, 0, 0, tiled=True)  10.4 us
    all_to_all x1, starting transfers between devices, layer(): incoming = lax.all_to_all(outgoing, TOK, 0, 0, tiled=True)  10.4 us
    all_to_all x1, waiting for transfers between devices, layer(): arrived = lax.all_to_all(sending, 'head', 0, 0, tiled=True)  8.92 us
    ppermute x2, starting transfers between devices, ring(): return lax.ppermute(x, axes, [(i, (i + step) % size) for i in range(size)])  6.48 us
  transfers between devices with their start and end apart: 12, of which 6 were waited for; matrix products, arithmetic and copies ran while one was open for 13% of the time, Pallas kernels for 0%

profile of v2, /device:TPU:1, one launch (start us, length us, event | category | flops | bytes accessed | tf_op | source)
XLA Modules:
  0.0 134.6 jit_solution(2294337475533772565)
XLA Ops:
  0.6 0.8 fusion.179
  1.4 0.7 maximum_maximum_fusion
  2.1 0.9 broadcast_in_dim.43
  3.1 16.5 %all-to-all-start = ((bf16[32,24,512]{2,1,0:T(8,128)(2,1)}), bf16[32,24,512]{2,1,0:T(8,128)(2,1)S(1)}, u32[]{:S(2)}, u32[]{:S(2)}) async-start(bf16[32,24,512]{2,1,0:T(8,128)(2,1)} %broadcast_in_dim.43), calls=%async_computation | async-start | bytes 1572864 | tf_op jit(solution)/shard_map/all_to_all | solution.py:35
  20.0 0.3 fusion.18
  20.7 0.3 fusion.20
  21.7 1.0 fusion.15
  23.0 0.6 fusion.169
  24.3 1.3 %fusion.165 = (s32[]{:T(128)}, s32[]{:T(128)}, s32[]{:T(128)}, s32[]{:T(128)}, s32[31]{0:T(128)S(1)}) fusion(s32[31]{0:T(128)S(1)} %copy-done.10, s32[]{:T(128)} %fusion.169, s32[]{:T(128)S(6)} %add.399, s32[31]{0:T(128)S(1)} %reduce.2), kind=kLoop, calls=%fused_computation.269 | loop fusion | flops 337 | bytes 396 | tf_op jit(solution)/shard_map/reduce_sum | solution.py:139
  26.4 0.5 subtract_convert_fusion
  28.3 1.1 subtract_select_fusion
  29.4 0.9 iota_compare_fusion.26
  30.3 0.3 fusion.16
  30.7 0.3 fusion.17
  31.3 12.1 %all-to-all-done = bf16[32,24,512]{2,1,0:T(8,128)(2,1)S(1)} async-done(((bf16[32,24,512]{2,1,0:T(8,128)(2,1)}), bf16[32,24,512]{2,1,0:T(8,128)(2,1)S(1)}, u32[]{:S(2)}, u32[]{:S(2)}) %all-to-all-start) | async-done | bytes 786464 | tf_op jit(solution)/shard_map/all_to_all | solution.py:35
  43.4 0.9 fusion.175
  44.4 1.9 %collective-permute-start = (bf16[16,24,512]{2,1,0:T(8,128)(2,1)}, bf16[16,24,512]{2,1,0:T(8,128)(2,1)}, u32[]{:S(2)}, u32[]{:S(2)}) collective-permute-start(bf16[16,24,512]{2,1,0:T(8,128)(2,1)} %get-tuple-element.22), channel_id=1, source_target_pairs={{0,8},{8,16},{16,24},{24,32},{32,40},{40,48},{48,56},{56,0},{1,9},... | collective-permute-start | bytes 1179656 | tf_op jit(solution)/shard_map/ppermute | solution.py:18
  46.3 4.6 %collective-permute-start.1 = (bf16[16,24,512]{2,1,0:T(8,128)(2,1)}, bf16[16,24,512]{2,1,0:T(8,128)(2,1)}, u32[]{:S(2)}, u32[]{:S(2)}) collective-permute-start(bf16[16,24,512]{2,1,0:T(8,128)(2,1)} %get-tuple-element.21), channel_id=1, source_target_pairs={{0,56},{8,0},{16,8},{24,16},{32,24},{40,32},{48,40},{56,48},{1,57}... | collective-permute-start | bytes 1179656 | tf_op jit(solution)/shard_map/ppermute | solution.py:18
  51.1 5.5 %collective-permute-start.2 = (bf16[32,24,512]{2,1,0:T(8,128)(2,1)S(1)}, bf16[32,24,512]{2,1,0:T(8,128)(2,1)S(1)}, u32[]{:S(2)}, u32[]{:S(2)}) collective-permute-start(bf16[32,24,512]{2,1,0:T(8,128)(2,1)S(1)} %all-to-all-done), channel_id=1, source_target_pairs={{0,4},{4,0},{1,5},{5,1},{2,6},{6,2},{3,7},{7,3},{8,12},{12,8},{9,1... | collective-permute-start | bytes 2359304 | tf_op jit(solution)/shard_map/ppermute | solution.py:22
  56.6 1.0 constant_dynamic-update-slice_fusion.1
  57.6 2.0 %collective-permute-done.1 = bf16[16,24,512]{2,1,0:T(8,128)(2,1)} collective-permute-done((bf16[16,24,512]{2,1,0:T(8,128)(2,1)}, bf16[16,24,512]{2,1,0:T(8,128)(2,1)}, u32[]{:S(2)}, u32[]{:S(2)}) %collective-permute-start.1) | collective-permute-done | bytes 393248 | tf_op jit(solution)/shard_map/ppermute | solution.py:18
  59.6 1.0 constant_dynamic-update-slice_fusion
  60.6 4.3 %collective-permute-start.3 = (bf16[32,24,512]{2,1,0:T(8,128)(2,1)S(1)}, bf16[32,24,512]{2,1,0:T(8,128)(2,1)S(1)}, u32[]{:S(2)}, u32[]{:S(2)}) collective-permute-start(bf16[32,24,512]{2,1,0:T(8,128)(2,1)S(1)} %constant_dynamic-update-slice_fusion), channel_id=1, source_target_pairs={{0,4},{4,0},{1,5},{5,1},{2,6},{6,2},{3,7},{7,3},{8,12},{12,8},{9,1... | collective-permute-start | bytes 2359304 | tf_op jit(solution)/shard_map/ppermute | solution.py:22
  65.5 1.2 collective-permute-done.3
  66.8 0.4 pad_maximum_fusion
  67.2 0.4 convolution_convert_fusion.7
  67.6 0.6 fusion.181
  68.2 0.6 copy-done
  69.3 4.9 %collective-permute-start.4 = (bf16[128,256]{1,0:T(8,128)(2,1)S(1)}, bf16[128,256]{1,0:T(8,128)(2,1)S(1)}, u32[]{:S(2)}, u32[]{:S(2)}) collective-permute-start(bf16[128,256]{1,0:T(8,128)(2,1)S(1)} %pad_maximum_fusion.8), channel_id=1, source_target_pairs={{0,32},{4,36},{8,40},{12,44},{16,48},{20,52},{24,56},{28,60},{32,6... | collective-permute-start | bytes 196616 | tf_op jit(solution)/shard_map/ppermute | solution.py:27
  74.2 3.9 %collective-permute-start.5 = (bf16[128,256]{1,0:T(8,128)(2,1)S(1)}, bf16[128,256]{1,0:T(8,128)(2,1)S(1)}, u32[]{:S(2)}, u32[]{:S(2)}) collective-permute-start(bf16[128,256]{1,0:T(8,128)(2,1)S(1)} %pad_maximum_fusion.8), channel_id=1, source_target_pairs={{0,24},{4,28},{8,32},{12,36},{16,40},{20,44},{24,48},{28,52},{32,5... | collective-permute-start | bytes 196616 | tf_op jit(solution)/shard_map/ppermute | solution.py:27
  78.2 4.1 %collective-permute-start.6 = (bf16[128,256]{1,0:T(8,128)(2,1)S(1)}, bf16[128,256]{1,0:T(8,128)(2,1)S(1)}, u32[]{:S(2)}, u32[]{:S(2)}) collective-permute-start(bf16[128,256]{1,0:T(8,128)(2,1)S(1)} %pad_maximum_fusion.8), channel_id=1, source_target_pairs={{0,16},{4,20},{8,24},{12,28},{16,32},{20,36},{24,40},{28,44},{32,4... | collective-permute-start | bytes 196616 | tf_op jit(solution)/shard_map/ppermute | solution.py:27
  82.3 2.7 %collective-permute-start.7 = (bf16[128,256]{1,0:T(8,128)(2,1)S(1)}, bf16[128,256]{1,0:T(8,128)(2,1)S(1)}, u32[]{:S(2)}, u32[]{:S(2)}) collective-permute-start(bf16[128,256]{1,0:T(8,128)(2,1)S(1)} %pad_maximum_fusion.8), channel_id=1, source_target_pairs={{0,8},{4,12},{8,16},{12,20},{16,24},{20,28},{24,32},{28,36},{32,40... | collective-permute-start | bytes 196616 | tf_op jit(solution)/shard_map/ppermute | solution.py:27
  85.0 2.9 %collective-permute-done.7 = bf16[128,256]{1,0:T(8,128)(2,1)S(1)} collective-permute-done((bf16[128,256]{1,0:T(8,128)(2,1)S(1)}, bf16[128,256]{1,0:T(8,128)(2,1)S(1)}, u32[]{:S(2)}, u32[]{:S(2)}) %collective-permute-start.7) | collective-permute-done | bytes 65568 | tf_op jit(solution)/shard_map/ppermute | solution.py:27
  87.9 2.9 %collective-permute-start.8 = (bf16[640,256]{1,0:T(8,128)(2,1)S(1)}, bf16[640,256]{1,0:T(8,128)(2,1)S(1)}, u32[]{:S(2)}, u32[]{:S(2)}) collective-permute-start(bf16[640,256]{1,0:T(8,128)(2,1)S(1)} %get-tuple-element.39), channel_id=1, source_target_pairs={{0,4},{4,0},{1,5},{5,1},{2,6},{6,2},{3,7},{7,3},{8,12},{12,8},{9,1... | collective-permute-start | bytes 983048 | tf_op jit(solution)/shard_map/ppermute | solution.py:22
  91.0 1.1 fusion.22
  92.1 10.4 %all-to-all-start.1 = ((bf16[128,8,128]{2,1,0:T(8,128)(2,1)}), bf16[128,8,128]{2,1,0:T(8,128)(2,1)S(1)}, u32[]{:S(2)}, u32[]{:S(2)}) async-start(bf16[128,8,128]{2,1,0:T(8,128)(2,1)} %fusion.22), calls=%async_computation.1 | async-start | bytes 524288 | tf_op jit(solution)/shard_map/all_to_all | solution.py:154
  102.7 0.6 fusion.180
  103.2 0.4 fusion.2
  103.7 0.5 fusion.23
  104.2 0.9 copy-done.1
  105.1 0.9 convolution_convert_fusion
  107.3 10.4 %all-to-all-done.1 = bf16[128,8,128]{2,1,0:T(8,128)(2,1)S(1)} async-done(((bf16[128,8,128]{2,1,0:T(8,128)(2,1)}), bf16[128,8,128]{2,1,0:T(8,128)(2,1)S(1)}, u32[]{:S(2)}, u32[]{:S(2)}) %all-to-all-start.1) | async-done | bytes 262176 | tf_op jit(solution)/shard_map/all_to_all | solution.py:154
  118.4 0.9 pad_maximum_fusion.3
  119.3 4.0 %all-to-all-start.2 = ((bf16[4,128,512]{2,1,0:T(8,128)(2,1)}), bf16[4,128,512]{2,1,0:T(8,128)(2,1)S(1)}, u32[]{:S(2)}, u32[]{:S(2)}) async-start(bf16[4,128,512]{2,1,0:T(8,128)(2,1)} %pad_maximum_fusion.3), calls=%async_computation.2 | async-start | bytes 1048576 | tf_op jit(solution)/shard_map/all_to_all | solution.py:231
  123.3 8.9 %all-to-all-done.2 = bf16[4,128,512]{2,1,0:T(8,128)(2,1)S(1)} async-done(((bf16[4,128,512]{2,1,0:T(8,128)(2,1)}), bf16[4,128,512]{2,1,0:T(8,128)(2,1)S(1)}, u32[]{:S(2)}, u32[]{:S(2)}) %all-to-all-start.2) | async-done | bytes 524320 | tf_op jit(solution)/shard_map/all_to_all | solution.py:231
  132.4 0.3 fusion.4
  132.8 1.1 copy.37
  133.9 0.7 add_convert_fusion
  (86 shorter events, 5.9 us)
Async XLA Ops:
  0.6 19.0 %copy-start.5 = (bf16[1536]{0:T(1024)(128)(2,1)S(1)}, bf16[1536]{0:T(1024)(128)(2,1)}, u32[]{:S(2)}) copy-start(bf16[1536]{0:T(1024)(128)(2,1)} %param.9) | copy-start | bytes 9220
  0.6 19.0 %copy-start.2 = (bf16[128,1536]{1,0:T(8,128)(2,1)S(1)}, bf16[128,1536]{1,0:T(8,128)(2,1)}, u32[]{:S(2)}) copy-start(bf16[128,1536]{1,0:T(8,128)(2,1)} %param.8) | copy-start | bytes 1179652
  3.1 40.4 %all-to-all-start = ((bf16[32,24,512]{2,1,0:T(8,128)(2,1)}), bf16[32,24,512]{2,1,0:T(8,128)(2,1)S(1)}, u32[]{:S(2)}, u32[]{:S(2)}) async-start(bf16[32,24,512]{2,1,0:T(8,128)(2,1)} %broadcast_in_dim.43), calls=%async_computation | async-start | bytes 1572864 | tf_op jit(solution)/shard_map/all_to_all | solution.py:35
  20.3 2.4 %copy-start.10 = (s32[31]{0:T(128)S(1)}, s32[31]{0:T(128)}, u32[]{:S(2)}) copy-start(s32[31]{0:T(128)} %param.14) | copy-start | bytes 376
  20.4 6.0 %copy-start.14 = (s32[128]{0:T(128)S(1)}, s32[128]{0:T(128)}, u32[]{:S(2)}) copy-start(s32[128]{0:T(128)} %param.13) | copy-start | bytes 1540
  23.0 7.6 %copy-start.11 = (s32[31]{0:T(128)}, s32[31]{0:T(128)S(1)}, u32[]{:S(2)}) copy-start(s32[31]{0:T(128)S(1)} %reduce.2) | copy-start | bytes 376
  26.4 1.9 %copy-start.6 = (s32[128]{0:T(128)}, s32[128]{0:T(128)S(1)}, u32[]{:S(2)}) copy-start(s32[128]{0:T(128)S(1)} %select_reduce_fusion) | copy-start | bytes 1540
  30.3 0.9 copy-start.3
  31.3 33.6 %copy-start.9 = (f32[128]{0:T(128)S(1)}, f32[128]{0:T(128)}, u32[]{:S(2)}) copy-start(f32[128]{0:T(128)} %get-tuple-element.67) | copy-start | bytes 1540
  31.3 33.9 %copy-start.7 = (s32[128]{0:T(128)S(1)}, s32[128]{0:T(128)}, u32[]{:S(2)}) copy-start(s32[128]{0:T(128)} %copy-done.6) | copy-start | bytes 1540
  31.3 33.9 %copy-start.8 = (s32[128]{0:T(128)S(1)}, s32[128]{0:T(128)}, u32[]{:S(2)}) copy-start(s32[128]{0:T(128)} %get-tuple-element.68) | copy-start | bytes 1540
  44.4 12.2 %collective-permute-start = (bf16[16,24,512]{2,1,0:T(8,128)(2,1)}, bf16[16,24,512]{2,1,0:T(8,128)(2,1)}, u32[]{:S(2)}, u32[]{:S(2)}) collective-permute-start(bf16[16,24,512]{2,1,0:T(8,128)(2,1)} %get-tuple-element.22), channel_id=1, source_target_pairs={{0,8},{8,16},{16,24},{24,32},{32,40},{40,48},{48,56},{56,0},{1,9},... | collective-permute-start | bytes 1179656 | tf_op jit(solution)/shard_map/ppermute | solution.py:18
  46.3 13.3 %collective-permute-start.1 = (bf16[16,24,512]{2,1,0:T(8,128)(2,1)}, bf16[16,24,512]{2,1,0:T(8,128)(2,1)}, u32[]{:S(2)}, u32[]{:S(2)}) collective-permute-start(bf16[16,24,512]{2,1,0:T(8,128)(2,1)} %get-tuple-element.21), channel_id=1, source_target_pairs={{0,56},{8,0},{16,8},{24,16},{32,24},{40,32},{48,40},{56,48},{1,57}... | collective-permute-start | bytes 1179656 | tf_op jit(solution)/shard_map/ppermute | solution.py:18
  51.1 14.4 %collective-permute-start.2 = (bf16[32,24,512]{2,1,0:T(8,128)(2,1)S(1)}, bf16[32,24,512]{2,1,0:T(8,128)(2,1)S(1)}, u32[]{:S(2)}, u32[]{:S(2)}) collective-permute-start(bf16[32,24,512]{2,1,0:T(8,128)(2,1)S(1)} %all-to-all-done), channel_id=1, source_target_pairs={{0,4},{4,0},{1,5},{5,1},{2,6},{6,2},{3,7},{7,3},{8,12},{12,8},{9,1... | collective-permute-start | bytes 2359304 | tf_op jit(solution)/shard_map/ppermute | solution.py:22
  60.6 6.1 %collective-permute-start.3 = (bf16[32,24,512]{2,1,0:T(8,128)(2,1)S(1)}, bf16[32,24,512]{2,1,0:T(8,128)(2,1)S(1)}, u32[]{:S(2)}, u32[]{:S(2)}) collective-permute-start(bf16[32,24,512]{2,1,0:T(8,128)(2,1)S(1)} %constant_dynamic-update-slice_fusion), channel_id=1, source_target_pairs={{0,4},{4,0},{1,5},{5,1},{2,6},{6,2},{3,7},{7,3},{8,12},{12,8},{9,1... | collective-permute-start | bytes 2359304 | tf_op jit(solution)/shard_map/ppermute | solution.py:22
  67.2 1.6 %copy-start = (bf16[4,4,8,24,512]{4,3,2,1,0:T(8,128)(2,1)}, bf16[4,4,8,24,512]{4,3,2,1,0:T(8,128)(2,1)S(1)}, u32[]{:S(2)}) copy-start(bf16[4,4,8,24,512]{4,3,2,1,0:T(8,128)(2,1)S(1)} %pad_maximum_fusion) | copy-start | bytes 9437188
  68.8 5.3 %copy-start.12 = (s32[31]{0:T(128)S(1)}, s32[31]{0:T(128)}, u32[]{:S(2)}) copy-start(s32[31]{0:T(128)} %copy-done.11) | copy-start | bytes 376
  68.8 22.2 %copy-start.4 = (pred[1024,128]{1,0:T(32,128)(4,1)S(1)}, pred[1024,128]{1,0:T(32,128)(4,1)}, u32[]{:S(2)}) copy-start(pred[1024,128]{1,0:T(32,128)(4,1)} %iota_compare_fusion.26) | copy-start | bytes 393220
  69.3 15.7 %collective-permute-start.4 = (bf16[128,256]{1,0:T(8,128)(2,1)S(1)}, bf16[128,256]{1,0:T(8,128)(2,1)S(1)}, u32[]{:S(2)}, u32[]{:S(2)}) collective-permute-start(bf16[128,256]{1,0:T(8,128)(2,1)S(1)} %pad_maximum_fusion.8), channel_id=1, source_target_pairs={{0,32},{4,36},{8,40},{12,44},{16,48},{20,52},{24,56},{28,60},{32,6... | collective-permute-start | bytes 196616 | tf_op jit(solution)/shard_map/ppermute | solution.py:27
  74.2 10.7 %collective-permute-start.5 = (bf16[128,256]{1,0:T(8,128)(2,1)S(1)}, bf16[128,256]{1,0:T(8,128)(2,1)S(1)}, u32[]{:S(2)}, u32[]{:S(2)}) collective-permute-start(bf16[128,256]{1,0:T(8,128)(2,1)S(1)} %pad_maximum_fusion.8), channel_id=1, source_target_pairs={{0,24},{4,28},{8,32},{12,36},{16,40},{20,44},{24,48},{28,52},{32,5... | collective-permute-start | bytes 196616 | tf_op jit(solution)/shard_map/ppermute | solution.py:27
  78.2 6.8 %collective-permute-start.6 = (bf16[128,256]{1,0:T(8,128)(2,1)S(1)}, bf16[128,256]{1,0:T(8,128)(2,1)S(1)}, u32[]{:S(2)}, u32[]{:S(2)}) collective-permute-start(bf16[128,256]{1,0:T(8,128)(2,1)S(1)} %pad_maximum_fusion.8), channel_id=1, source_target_pairs={{0,16},{4,20},{8,24},{12,28},{16,32},{20,36},{24,40},{28,44},{32,4... | collective-permute-start | bytes 196616 | tf_op jit(solution)/shard_map/ppermute | solution.py:27
  82.3 5.6 %collective-permute-start.7 = (bf16[128,256]{1,0:T(8,128)(2,1)S(1)}, bf16[128,256]{1,0:T(8,128)(2,1)S(1)}, u32[]{:S(2)}, u32[]{:S(2)}) collective-permute-start(bf16[128,256]{1,0:T(8,128)(2,1)S(1)} %pad_maximum_fusion.8), channel_id=1, source_target_pairs={{0,8},{4,12},{8,16},{12,20},{16,24},{20,28},{24,32},{28,36},{32,40... | collective-permute-start | bytes 196616 | tf_op jit(solution)/shard_map/ppermute | solution.py:27
  87.9 14.6 %collective-permute-start.8 = (bf16[640,256]{1,0:T(8,128)(2,1)S(1)}, bf16[640,256]{1,0:T(8,128)(2,1)S(1)}, u32[]{:S(2)}, u32[]{:S(2)}) collective-permute-start(bf16[640,256]{1,0:T(8,128)(2,1)S(1)} %get-tuple-element.39), channel_id=1, source_target_pairs={{0,4},{4,0},{1,5},{5,1},{2,6},{6,2},{3,7},{7,3},{8,12},{12,8},{9,1... | collective-permute-start | bytes 983048 | tf_op jit(solution)/shard_map/ppermute | solution.py:22
  92.1 25.6 %all-to-all-start.1 = ((bf16[128,8,128]{2,1,0:T(8,128)(2,1)}), bf16[128,8,128]{2,1,0:T(8,128)(2,1)S(1)}, u32[]{:S(2)}, u32[]{:S(2)}) async-start(bf16[128,8,128]{2,1,0:T(8,128)(2,1)} %fusion.22), calls=%async_computation.1 | async-start | bytes 524288 | tf_op jit(solution)/shard_map/all_to_all | solution.py:154
  103.2 1.9 %copy-start.1 = (bf16[4,4,8,24,512]{4,3,2,1,0:T(8,128)(2,1)S(1)}, bf16[4,4,8,24,512]{4,3,2,1,0:T(8,128)(2,1)}, u32[]{:S(2)}) copy-start(bf16[4,4,8,24,512]{4,3,2,1,0:T(8,128)(2,1)} %copy-done) | copy-start | bytes 9437188
  118.4 14.0 %copy-start.13 = (s32[96]{0:T(128)S(1)}, s32[96]{0:T(128)}, u32[]{:S(2)}) copy-start(s32[96]{0:T(128)} %param.15) | copy-start | bytes 1156
  119.3 12.9 %all-to-all-start.2 = ((bf16[4,128,512]{2,1,0:T(8,128)(2,1)}), bf16[4,128,512]{2,1,0:T(8,128)(2,1)S(1)}, u32[]{:S(2)}, u32[]{:S(2)}) async-start(bf16[4,128,512]{2,1,0:T(8,128)(2,1)} %pad_maximum_fusion.3), calls=%async_computation.2 | async-start | bytes 1048576 | tf_op jit(solution)/shard_map/all_to_all | solution.py:231

commit v3 on v2

--- a/solution.py
+++ b/solution.py
@@ -13,11 +13,6 @@
 F32 = jnp.float32
 
 
-def ring(x, axes, step):
-    size = lax.axis_size(axes)
-    return lax.ppermute(x, axes, [(i, (i + step) % size) for i in range(size)])
-
-
 def swap(x):
     return lax.ppermute(x, "c", [(0, 1), (1, 0)])
 
@@ -28,33 +23,54 @@
 
 
 def gather_rows(chunk):
-    line = ("zh", "zl", "yh")
+    line = ("zh", "zl", "c")
     members = lax.axis_size(line)
     n_zh = lax.axis_size("zh")
+    n_y = lax.axis_size(("yh", "yl"))
     half = members // 2
+    core = lax.axis_index("c")
     own = lax.all_to_all(
         jnp.broadcast_to(chunk[None], (members,) + chunk.shape), line, 0, 0, tiled=True
     )
-    below = ring(own[:half], ("yh", "yl"), 1)
-    above = ring(own[half:], ("yh", "yl"), -1)
-    own_swapped = swap(own)
-    sides = jnp.concatenate([below, above], axis=0)
-    sides_swapped = swap(sides)
+    route = [(2 * y, 2 * ((y + 1) % n_y)) for y in range(n_y)]
+    route += [(2 * y + 1, 2 * ((y - 1) % n_y) + 1) for y in range(n_y)]
+
+    def onward(block):
+        return lax.ppermute(block, ("yh", "yl", "c"), route)
+
+    moving = own
+    walked, swapped = [], []
+    for _ in range(n_y // 2 - 1):
+        moving = onward(moving)
+        walked.append(moving)
+        swapped.append(swap(moving))
+    last = onward(lax.dynamic_slice_in_dim(moving, core * half, half, 0))
+    last_swapped = swap(last)
+    far = jnp.concatenate(
+        [
+            jnp.where(core == 0, last, last_swapped),
+            jnp.where(core == 0, last_swapped, last),
+        ],
+        axis=0,
+    )
     shape = (n_zh, members // n_zh) + chunk.shape
-    pieces = [piece.reshape(shape) for piece in (own, sides, own_swapped, sides_swapped)]
+    pieces = [piece.reshape(shape) for piece in [own] + walked + swapped + [far]]
     return jnp.stack(pieces, axis=1)
 
 
 def block_places(rows, offset, stacked):
-    yl, core = lax.axis_index("yl"), lax.axis_index("c")
-    n_zl, n_yh = lax.axis_size("zl"), lax.axis_size("yh")
-    place = jnp.arange(4 * n_zl * n_yh * stacked, dtype=jnp.int32)
+    core = lax.axis_index("c")
+    here = lax.axis_index(("yh", "yl"))
+    n_zl, n_y = lax.axis_size("zl"), lax.axis_size(("yh", "yl"))
+    steps = n_y // 2 - 1
+    place = jnp.arange(n_y * n_zl * 2 * stacked, dtype=jnp.int32)
     row = place % stacked - offset
-    yh = (place // stacked) % n_yh
-    zl = (place // (stacked * n_yh)) % n_zl
-    piece = place // (stacked * n_yh * n_zl)
-    y = 2 * yh + (yl ^ (piece % 2))
-    device = (zl * (2 * n_yh) + y) * 2 + (core ^ (piece // 2))
+    of_core = (place // stacked) % 2
+    zl = (place // (stacked * 2)) % n_zl
+    piece = place // (stacked * 2 * n_zl)
+    distance = jnp.where(piece <= steps, -piece, piece - steps)
+    y = (here + jnp.where(core == 0, distance, -distance)) % n_y
+    device = (zl * n_y + y) * 2 + of_core
     return jnp.where((row >= 0) & (row < rows), device * rows + row, -1)
 
 

time: 135 us -> 149 us (1.10)
  starting transfers between devices: 65.6 us -> 79.3 us
  waiting for transfers between devices: 37.5 us -> 33.5 us
  other arithmetic: 9.92 us -> 12.8 us
    all_to_all x1, waiting for transfers between devices: 12.1 us -> 0.01 us  [gather_rows(): lax.all_to_all(jnp.broadcast_to(chunk[None], (members,) + chunk.shape), l...]
    ppermute x2 -> x4, starting transfers between devices: 6.48 us -> 17.5 us  [onward(): return lax.ppermute(block, ('yh', 'yl', 'c'), route)]
    ppermute x2 -> x4, waiting for transfers between devices: 1.98 us -> 12 us  [onward(): return lax.ppermute(block, ('yh', 'yl', 'c'), route)]
    all_to_all x1, starting transfers between devices: 16.5 us -> 11.8 us  [gather_rows(): lax.all_to_all(jnp.broadcast_to(chunk[None], (members,) + chunk.shape), l...]
    all_to_all x1, starting transfers between devices: 10.4 us -> 14.7 us  [layer(): incoming = lax.all_to_all(outgoing, TOK, 0, 0, tiled=True)]
    ppermute x3 -> x5, starting transfers between devices: 12.7 us -> 16.6 us  [swap(): return lax.ppermute(x, 'c', [(0, 1), (1, 0)])]
    ppermute x4, waiting for transfers between devices: 2.9 us -> 1.24 us  [earlier(): lax.ppermute(x, TOK, [(i, i + distance) for i in range(size - distance)])]
    unnamed x36 -> x38, local copies, waits for them, and re-layouts: 3.7 us -> 5.12 us
  transfers between devices with their start and end apart: 12 -> 16, of which waited for: 6 -> 7; matrix products, arithmetic and copies ran while one was open for 13% -> 15% of each run, Pallas kernels for 0% -> 0%
where the time goes in v3:
time: 149 us; the launch traced here: 148 us
  starting transfers between devices  79.3 us (53%)
  waiting for transfers between devices  33.5 us (22%)
  other arithmetic  12.8 us (9%)
  matrix products  9.99 us (7%)
  local copies, waits for them, and re-layouts  8.2 us (6%)
  between operations  3.96 us (3%)
    ppermute x4, starting transfers between devices, onward(): return lax.ppermute(block, ('yh', 'yl', 'c'), route)  17.5 us
    ppermute x5, starting transfers between devices, swap(): return lax.ppermute(x, 'c', [(0, 1), (1, 0)])  16.6 us
    all_to_all x1, starting transfers between devices, layer(): incoming = lax.all_to_all(outgoing, TOK, 0, 0, tiled=True)  14.7 us
    ppermute x4, starting transfers between devices, earlier(): lax.ppermute(x, TOK, [(i, i + distance) for i in range(size - distance)])  14.7 us
    ppermute x4, waiting for transfers between devices, onward(): return lax.ppermute(block, ('yh', 'yl', 'c'), route)  12 us
    all_to_all x1, starting transfers between devices, gather_rows(): lax.all_to_all(jnp.broadcast_to(chunk[None], (members,) + chunk.shape), l...  11.8 us
    all_to_all x1, waiting for transfers between devices, layer(): incoming = lax.all_to_all(outgoing, TOK, 0, 0, tiled=True)  10.4 us
    all_to_all x1, waiting for transfers between devices, layer(): arrived = lax.all_to_all(sending, 'head', 0, 0, tiled=True)  8.92 us
  transfers between devices with their start and end apart: 16, of which 7 were waited for; matrix products, arithmetic and copies ran while one was open for 15% of the time, Pallas kernels for 0%

profile of v3, /device:TPU:1, one launch (start us, length us, event | category | flops | bytes accessed | tf_op | source)
XLA Modules:
  0.0 147.8 jit_solution(4147102508086251746)
XLA Ops:
  0.6 0.8 fusion.172
  1.4 0.7 maximum_maximum_fusion
  2.1 0.8 broadcast_in_dim.43
  2.9 11.8 %all-to-all-start = ((bf16[16,24,512]{2,1,0:T(8,128)(2,1)}), bf16[16,24,512]{2,1,0:T(8,128)(2,1)S(1)}, u32[]{:S(2)}, u32[]{:S(2)}) async-start(bf16[16,24,512]{2,1,0:T(8,128)(2,1)} %broadcast_in_dim.43), calls=%async_computation | async-start | bytes 786432 | tf_op jit(solution)/shard_map/all_to_all | solution.py:32
  14.7 0.7 copy.30
  15.7 0.6 fusion.163
  16.9 2.0 %fusion.159 = (s32[]{:T(128)}, s32[]{:T(128)}, s32[]{:T(128)}, s32[]{:T(128)}, s32[31]{0:T(128)S(1)}) fusion(s32[31]{0:T(128)} %param.14, s32[]{:T(128)} %fusion.163, s32[]{:T(128)S(6)} %add.413, s32[31]{0:T(128)S(1)} %reduce.2), kind=kLoop, calls=%fused_computation.270 | loop fusion | flops 337 | bytes 396 | tf_op jit(solution)/shard_map/reduce_sum | solution.py:155
  19.6 0.7 convert_element_type.101
  20.3 1.2 fusion.30
  23.8 1.0 fusion.19
  24.8 1.0 fusion.18
  27.2 1.0 fusion.92
  28.2 1.2 subtract_select_fusion
  29.9 5.2 %collective-permute-start = (bf16[16,24,512]{2,1,0:T(8,128)(2,1)S(1)}, bf16[16,24,512]{2,1,0:T(8,128)(2,1)S(1)}, u32[]{:S(2)}, u32[]{:S(2)}) collective-permute-start(bf16[16,24,512]{2,1,0:T(8,128)(2,1)S(1)} %all-to-all-done), channel_id=1, source_target_pairs={{0,8},{8,16},{16,24},{24,32},{32,40},{40,48},{48,56},{56,0},{4,60}... | collective-permute-start | bytes 1179656 | tf_op jit(solution)/shard_map/ppermute | solution.py:39
  35.1 0.9 iota_compare_fusion.26
  36.0 3.8 %collective-permute-done = bf16[16,24,512]{2,1,0:T(8,128)(2,1)S(1)} collective-permute-done((bf16[16,24,512]{2,1,0:T(8,128)(2,1)S(1)}, bf16[16,24,512]{2,1,0:T(8,128)(2,1)S(1)}, u32[]{:S(2)}, u32[]{:S(2)}) %collective-permute-start) | collective-permute-done | bytes 393248 | tf_op jit(solution)/shard_map/ppermute | solution.py:39
  39.8 5.0 %collective-permute-start.1 = (bf16[16,24,512]{2,1,0:T(8,128)(2,1)S(1)}, bf16[16,24,512]{2,1,0:T(8,128)(2,1)}, u32[]{:S(2)}, u32[]{:S(2)}) collective-permute-start(bf16[16,24,512]{2,1,0:T(8,128)(2,1)S(1)} %collective-permute-done), channel_id=1, source_target_pairs={{0,8},{8,16},{16,24},{24,32},{32,40},{40,48},{48,56},{56,0},{4,60}... | collective-permute-start | bytes 1179656 | tf_op jit(solution)/shard_map/ppermute | solution.py:39
  44.8 0.9 iota_compare_fusion.27
  45.8 3.8 %collective-permute-done.1 = bf16[16,24,512]{2,1,0:T(8,128)(2,1)} collective-permute-done((bf16[16,24,512]{2,1,0:T(8,128)(2,1)S(1)}, bf16[16,24,512]{2,1,0:T(8,128)(2,1)}, u32[]{:S(2)}, u32[]{:S(2)}) %collective-permute-start.1) | collective-permute-done | bytes 393248 | tf_op jit(solution)/shard_map/ppermute | solution.py:39
  49.5 5.1 %collective-permute-start.2 = (bf16[16,24,512]{2,1,0:T(8,128)(2,1)}, bf16[16,24,512]{2,1,0:T(8,128)(2,1)S(1)}, u32[]{:S(2)}, u32[]{:S(2)}) collective-permute-start(bf16[16,24,512]{2,1,0:T(8,128)(2,1)} %collective-permute-done.1), channel_id=1, source_target_pairs={{0,8},{8,16},{16,24},{24,32},{32,40},{40,48},{48,56},{56,0},{4,60}... | collective-permute-start | bytes 1179656 | tf_op jit(solution)/shard_map/ppermute | solution.py:39
  54.7 1.9 %collective-permute-start.3 = (bf16[16,24,512]{2,1,0:T(8,128)(2,1)}, bf16[16,24,512]{2,1,0:T(8,128)(2,1)S(1)}, u32[]{:S(2)}, u32[]{:S(2)}) collective-permute-start(bf16[16,24,512]{2,1,0:T(8,128)(2,1)} %copy-done.4), channel_id=1, source_target_pairs={{0,4},{4,0},{1,5},{5,1},{2,6},{6,2},{3,7},{7,3},{8,12},{12,8},{9,1... | collective-permute-start | bytes 1179656 | tf_op jit(solution)/shard_map/ppermute | solution.py:17
  56.6 1.0 constant_dynamic-update-slice_fusion.6
  57.7 2.4 %collective-permute-start.4 = (bf16[16,24,512]{2,1,0:T(8,128)(2,1)}, bf16[16,24,512]{2,1,0:T(8,128)(2,1)S(1)}, u32[]{:S(2)}, u32[]{:S(2)}) collective-permute-start(bf16[16,24,512]{2,1,0:T(8,128)(2,1)} %collective-permute-done.1), channel_id=1, source_target_pairs={{0,4},{4,0},{1,5},{5,1},{2,6},{6,2},{3,7},{7,3},{8,12},{12,8},{9,1... | collective-permute-start | bytes 1179656 | tf_op jit(solution)/shard_map/ppermute | solution.py:17
  60.1 1.0 constant_dynamic-update-slice_fusion.5
  61.1 4.1 %collective-permute-start.5 = (bf16[16,24,512]{2,1,0:T(8,128)(2,1)S(1)}, bf16[16,24,512]{2,1,0:T(8,128)(2,1)S(1)}, u32[]{:S(2)}, u32[]{:S(2)}) collective-permute-start(bf16[16,24,512]{2,1,0:T(8,128)(2,1)S(1)} %collective-permute-done.2), channel_id=1, source_target_pairs={{0,4},{4,0},{1,5},{5,1},{2,6},{6,2},{3,7},{7,3},{8,12},{12,8},{9,1... | collective-permute-start | bytes 1179656 | tf_op jit(solution)/shard_map/ppermute | solution.py:17
  65.2 2.2 %collective-permute-start.6 = (bf16[8,24,512]{2,1,0:T(8,128)(2,1)S(1)}, bf16[8,24,512]{2,1,0:T(8,128)(2,1)S(1)}, u32[]{:S(2)}, u32[]{:S(2)}) collective-permute-start(bf16[8,24,512]{2,1,0:T(8,128)(2,1)S(1)} %constant_dynamic-slice_fusion), channel_id=1, source_target_pairs={{0,8},{8,16},{16,24},{24,32},{32,40},{40,48},{48,56},{56,0},{4,60}... | collective-permute-start | bytes 589832 | tf_op jit(solution)/shard_map/ppermute | solution.py:39
  67.5 4.5 %collective-permute-done.6 = bf16[8,24,512]{2,1,0:T(8,128)(2,1)S(1)} collective-permute-done((bf16[8,24,512]{2,1,0:T(8,128)(2,1)S(1)}, bf16[8,24,512]{2,1,0:T(8,128)(2,1)S(1)}, u32[]{:S(2)}, u32[]{:S(2)}) %collective-permute-start.6) | collective-permute-done | bytes 196640 | tf_op jit(solution)/shard_map/ppermute | solution.py:39
  71.9 4.0 %collective-permute-start.7 = (bf16[8,24,512]{2,1,0:T(8,128)(2,1)S(1)}, bf16[8,24,512]{2,1,0:T(8,128)(2,1)S(1)}, u32[]{:S(2)}, u32[]{:S(2)}) collective-permute-start(bf16[8,24,512]{2,1,0:T(8,128)(2,1)S(1)} %collective-permute-done.6), channel_id=1, source_target_pairs={{0,4},{4,0},{1,5},{5,1},{2,6},{6,2},{3,7},{7,3},{8,12},{12,8},{9,1... | collective-permute-start | bytes 589832 | tf_op jit(solution)/shard_map/ppermute | solution.py:17
  76.0 1.0 collective-permute-done.7
  77.1 0.6 fusion.174
  77.9 0.9 copy-done
  79.4 7.2 %collective-permute-start.8 = (bf16[128,256]{1,0:T(8,128)(2,1)S(1)}, bf16[128,256]{1,0:T(8,128)(2,1)S(1)}, u32[]{:S(2)}, u32[]{:S(2)}) collective-permute-start(bf16[128,256]{1,0:T(8,128)(2,1)S(1)} %pad_maximum_fusion.8), channel_id=1, source_target_pairs={{0,32},{4,36},{8,40},{12,44},{16,48},{20,52},{24,56},{28,60},{32,6... | collective-permute-start | bytes 196616 | tf_op jit(solution)/shard_map/ppermute | solution.py:22
  86.7 1.3 collective-permute-start.9
  88.0 2.5 %collective-permute-start.10 = (bf16[128,256]{1,0:T(8,128)(2,1)S(1)}, bf16[128,256]{1,0:T(8,128)(2,1)S(1)}, u32[]{:S(2)}, u32[]{:S(2)}) collective-permute-start(bf16[128,256]{1,0:T(8,128)(2,1)S(1)} %pad_maximum_fusion.8), channel_id=1, source_target_pairs={{0,16},{4,20},{8,24},{12,28},{16,32},{20,36},{24,40},{28,44},{32,4... | collective-permute-start | bytes 196616 | tf_op jit(solution)/shard_map/ppermute | solution.py:22
  90.5 3.7 %collective-permute-start.11 = (bf16[128,256]{1,0:T(8,128)(2,1)S(1)}, bf16[128,256]{1,0:T(8,128)(2,1)S(1)}, u32[]{:S(2)}, u32[]{:S(2)}) collective-permute-start(bf16[128,256]{1,0:T(8,128)(2,1)S(1)} %pad_maximum_fusion.8), channel_id=1, source_target_pairs={{0,8},{4,12},{8,16},{12,20},{16,24},{20,28},{24,32},{28,36},{32,40... | collective-permute-start | bytes 196616 | tf_op jit(solution)/shard_map/ppermute | solution.py:22
  94.3 1.2 collective-permute-done.11
  95.6 4.2 %collective-permute-start.12 = (bf16[640,256]{1,0:T(8,128)(2,1)S(1)}, bf16[640,256]{1,0:T(8,128)(2,1)S(1)}, u32[]{:S(2)}, u32[]{:S(2)}) collective-permute-start(bf16[640,256]{1,0:T(8,128)(2,1)S(1)} %get-tuple-element.39), channel_id=1, source_target_pairs={{0,4},{4,0},{1,5},{5,1},{2,6},{6,2},{3,7},{7,3},{8,12},{12,8},{9,1... | collective-permute-start | bytes 983048 | tf_op jit(solution)/shard_map/ppermute | solution.py:17
  99.9 1.1 fusion.22
  101.0 14.7 %all-to-all-start.1 = ((bf16[128,8,128]{2,1,0:T(8,128)(2,1)}), bf16[128,8,128]{2,1,0:T(8,128)(2,1)S(1)}, u32[]{:S(2)}, u32[]{:S(2)}) async-start(bf16[128,8,128]{2,1,0:T(8,128)(2,1)} %fusion.22), calls=%async_computation.1 | async-start | bytes 524288 | tf_op jit(solution)/shard_map/all_to_all | solution.py:170
  115.9 0.6 fusion.173
  117.4 0.9 copy-done.1
  118.3 0.9 convolution_convert_fusion
  120.5 10.4 %all-to-all-done.1 = bf16[128,8,128]{2,1,0:T(8,128)(2,1)S(1)} async-done(((bf16[128,8,128]{2,1,0:T(8,128)(2,1)}), bf16[128,8,128]{2,1,0:T(8,128)(2,1)S(1)}, u32[]{:S(2)}, u32[]{:S(2)}) %all-to-all-start.1) | async-done | bytes 262176 | tf_op jit(solution)/shard_map/all_to_all | solution.py:170
  131.6 0.9 pad_maximum_fusion.2
  132.5 4.0 %all-to-all-start.2 = ((bf16[4,128,512]{2,1,0:T(8,128)(2,1)}), bf16[4,128,512]{2,1,0:T(8,128)(2,1)S(1)}, u32[]{:S(2)}, u32[]{:S(2)}) async-start(bf16[4,128,512]{2,1,0:T(8,128)(2,1)} %pad_maximum_fusion.2), calls=%async_computation.2 | async-start | bytes 1048576 | tf_op jit(solution)/shard_map/all_to_all | solution.py:247
  136.5 8.9 %all-to-all-done.2 = bf16[4,128,512]{2,1,0:T(8,128)(2,1)S(1)} async-done(((bf16[4,128,512]{2,1,0:T(8,128)(2,1)}), bf16[4,128,512]{2,1,0:T(8,128)(2,1)S(1)}, u32[]{:S(2)}, u32[]{:S(2)}) %all-to-all-start.2) | async-done | bytes 524320 | tf_op jit(solution)/shard_map/all_to_all | solution.py:247
  146.0 1.1 copy.37
  147.1 0.7 add_convert_fusion
  (97 shorter events, 8.1 us)
Async XLA Ops:
  0.6 20.9 %copy-start.2 = (bf16[128,1536]{1,0:T(8,128)(2,1)S(1)}, bf16[128,1536]{1,0:T(8,128)(2,1)}, u32[]{:S(2)}) copy-start(bf16[128,1536]{1,0:T(8,128)(2,1)} %param.8) | copy-start | bytes 1179652
  2.9 26.9 %all-to-all-start = ((bf16[16,24,512]{2,1,0:T(8,128)(2,1)}), bf16[16,24,512]{2,1,0:T(8,128)(2,1)S(1)}, u32[]{:S(2)}, u32[]{:S(2)}) async-start(bf16[16,24,512]{2,1,0:T(8,128)(2,1)} %broadcast_in_dim.43), calls=%async_computation | async-start | bytes 786432 | tf_op jit(solution)/shard_map/all_to_all | solution.py:32
  22.4 4.7 %copy-start.12 = (s32[128]{0:T(128)S(1)}, s32[128]{0:T(128)}, u32[]{:S(2)}) copy-start(s32[128]{0:T(128)} %param.13) | copy-start | bytes 1540
  29.9 15.8 %copy-start.7 = (bf16[128,768]{1,0:T(8,128)(2,1)S(1)}, bf16[128,768]{1,0:T(8,128)(2,1)}, u32[]{:S(2)}) copy-start(bf16[128,768]{1,0:T(8,128)(2,1)} %fusion.19) | copy-start | bytes 589828
  29.9 15.8 %copy-start.8 = (bf16[128,768]{1,0:T(8,128)(2,1)S(1)}, bf16[128,768]{1,0:T(8,128)(2,1)}, u32[]{:S(2)}) copy-start(bf16[128,768]{1,0:T(8,128)(2,1)} %fusion.18) | copy-start | bytes 589828
  29.9 9.9 %collective-permute-start = (bf16[16,24,512]{2,1,0:T(8,128)(2,1)S(1)}, bf16[16,24,512]{2,1,0:T(8,128)(2,1)S(1)}, u32[]{:S(2)}, u32[]{:S(2)}) collective-permute-start(bf16[16,24,512]{2,1,0:T(8,128)(2,1)S(1)} %all-to-all-done), channel_id=1, source_target_pairs={{0,8},{8,16},{16,24},{24,32},{32,40},{40,48},{48,56},{56,0},{4,60}... | collective-permute-start | bytes 1179656 | tf_op jit(solution)/shard_map/ppermute | solution.py:39
  39.8 6.0 %copy-start.4 = (bf16[16,24,512]{2,1,0:T(8,128)(2,1)}, bf16[16,24,512]{2,1,0:T(8,128)(2,1)S(1)}, u32[]{:S(2)}) copy-start(bf16[16,24,512]{2,1,0:T(8,128)(2,1)S(1)} %collective-permute-done) | copy-start | bytes 1179652
  39.8 9.7 %collective-permute-start.1 = (bf16[16,24,512]{2,1,0:T(8,128)(2,1)S(1)}, bf16[16,24,512]{2,1,0:T(8,128)(2,1)}, u32[]{:S(2)}, u32[]{:S(2)}) collective-permute-start(bf16[16,24,512]{2,1,0:T(8,128)(2,1)S(1)} %collective-permute-done), channel_id=1, source_target_pairs={{0,8},{8,16},{16,24},{24,32},{32,40},{40,48},{48,56},{56,0},{4,60}... | collective-permute-start | bytes 1179656 | tf_op jit(solution)/shard_map/ppermute | solution.py:39
  49.5 11.6 %collective-permute-start.2 = (bf16[16,24,512]{2,1,0:T(8,128)(2,1)}, bf16[16,24,512]{2,1,0:T(8,128)(2,1)S(1)}, u32[]{:S(2)}, u32[]{:S(2)}) collective-permute-start(bf16[16,24,512]{2,1,0:T(8,128)(2,1)} %collective-permute-done.1), channel_id=1, source_target_pairs={{0,8},{8,16},{16,24},{24,32},{32,40},{40,48},{48,56},{56,0},{4,60}... | collective-permute-start | bytes 1179656 | tf_op jit(solution)/shard_map/ppermute | solution.py:39
  54.7 12.7 %collective-permute-start.3 = (bf16[16,24,512]{2,1,0:T(8,128)(2,1)}, bf16[16,24,512]{2,1,0:T(8,128)(2,1)S(1)}, u32[]{:S(2)}, u32[]{:S(2)}) collective-permute-start(bf16[16,24,512]{2,1,0:T(8,128)(2,1)} %copy-done.4), channel_id=1, source_target_pairs={{0,4},{4,0},{1,5},{5,1},{2,6},{6,2},{3,7},{7,3},{8,12},{12,8},{9,1... | collective-permute-start | bytes 1179656 | tf_op jit(solution)/shard_map/ppermute | solution.py:17
  57.7 18.3 %collective-permute-start.4 = (bf16[16,24,512]{2,1,0:T(8,128)(2,1)}, bf16[16,24,512]{2,1,0:T(8,128)(2,1)S(1)}, u32[]{:S(2)}, u32[]{:S(2)}) collective-permute-start(bf16[16,24,512]{2,1,0:T(8,128)(2,1)} %collective-permute-done.1), channel_id=1, source_target_pairs={{0,4},{4,0},{1,5},{5,1},{2,6},{6,2},{3,7},{7,3},{8,12},{12,8},{9,1... | collective-permute-start | bytes 1179656 | tf_op jit(solution)/shard_map/ppermute | solution.py:17
  61.1 14.9 %collective-permute-start.5 = (bf16[16,24,512]{2,1,0:T(8,128)(2,1)S(1)}, bf16[16,24,512]{2,1,0:T(8,128)(2,1)S(1)}, u32[]{:S(2)}, u32[]{:S(2)}) collective-permute-start(bf16[16,24,512]{2,1,0:T(8,128)(2,1)S(1)} %collective-permute-done.2), channel_id=1, source_target_pairs={{0,4},{4,0},{1,5},{5,1},{2,6},{6,2},{3,7},{7,3},{8,12},{12,8},{9,1... | collective-permute-start | bytes 1179656 | tf_op jit(solution)/shard_map/ppermute | solution.py:17
  65.2 6.7 %collective-permute-start.6 = (bf16[8,24,512]{2,1,0:T(8,128)(2,1)S(1)}, bf16[8,24,512]{2,1,0:T(8,128)(2,1)S(1)}, u32[]{:S(2)}, u32[]{:S(2)}) collective-permute-start(bf16[8,24,512]{2,1,0:T(8,128)(2,1)S(1)} %constant_dynamic-slice_fusion), channel_id=1, source_target_pairs={{0,8},{8,16},{16,24},{24,32},{32,40},{40,48},{48,56},{56,0},{4,60}... | collective-permute-start | bytes 589832 | tf_op jit(solution)/shard_map/ppermute | solution.py:39
  71.9 5.0 %collective-permute-start.7 = (bf16[8,24,512]{2,1,0:T(8,128)(2,1)S(1)}, bf16[8,24,512]{2,1,0:T(8,128)(2,1)S(1)}, u32[]{:S(2)}, u32[]{:S(2)}) collective-permute-start(bf16[8,24,512]{2,1,0:T(8,128)(2,1)S(1)} %collective-permute-done.6), channel_id=1, source_target_pairs={{0,4},{4,0},{1,5},{5,1},{2,6},{6,2},{3,7},{7,3},{8,12},{12,8},{9,1... | collective-permute-start | bytes 589832 | tf_op jit(solution)/shard_map/ppermute | solution.py:17
  77.1 1.6 %copy-start = (bf16[4,8,4,24,512]{4,3,2,1,0:T(8,128)(2,1)}, bf16[4,8,4,24,512]{4,3,2,1,0:T(8,128)(2,1)S(1)}, u32[]{:S(2)}) copy-start(bf16[4,8,4,24,512]{4,3,2,1,0:T(8,128)(2,1)S(1)} %constant_dynamic-update-slice_fusion) | copy-start | bytes 9437188
  77.7 1.4 copy-start.3
  77.7 1.4 copy-start.5
  77.7 1.4 copy-start.6
  78.7 21.2 %copy-start.9 = (pred[1024,128]{1,0:T(32,128)(4,1)S(1)}, pred[1024,128]{1,0:T(32,128)(4,1)}, u32[]{:S(2)}) copy-start(pred[1024,128]{1,0:T(32,128)(4,1)} %iota_compare_fusion.26) | copy-start | bytes 393220
  78.7 21.2 %copy-start.10 = (pred[1024,128]{1,0:T(32,128)(4,1)S(1)}, pred[1024,128]{1,0:T(32,128)(4,1)}, u32[]{:S(2)}) copy-start(pred[1024,128]{1,0:T(32,128)(4,1)} %iota_compare_fusion.27) | copy-start | bytes 393220
  79.4 14.8 %collective-permute-start.8 = (bf16[128,256]{1,0:T(8,128)(2,1)S(1)}, bf16[128,256]{1,0:T(8,128)(2,1)S(1)}, u32[]{:S(2)}, u32[]{:S(2)}) collective-permute-start(bf16[128,256]{1,0:T(8,128)(2,1)S(1)} %pad_maximum_fusion.8), channel_id=1, source_target_pairs={{0,32},{4,36},{8,40},{12,44},{16,48},{20,52},{24,56},{28,60},{32,6... | collective-permute-start | bytes 196616 | tf_op jit(solution)/shard_map/ppermute | solution.py:22
  86.7 7.5 %collective-permute-start.9 = (bf16[128,256]{1,0:T(8,128)(2,1)S(1)}, bf16[128,256]{1,0:T(8,128)(2,1)S(1)}, u32[]{:S(2)}, u32[]{:S(2)}) collective-permute-start(bf16[128,256]{1,0:T(8,128)(2,1)S(1)} %pad_maximum_fusion.8), channel_id=1, source_target_pairs={{0,24},{4,28},{8,32},{12,36},{16,40},{20,44},{24,48},{28,52},{32,5... | collective-permute-start | bytes 196616 | tf_op jit(solution)/shard_map/ppermute | solution.py:22
  88.0 6.3 %collective-permute-start.10 = (bf16[128,256]{1,0:T(8,128)(2,1)S(1)}, bf16[128,256]{1,0:T(8,128)(2,1)S(1)}, u32[]{:S(2)}, u32[]{:S(2)}) collective-permute-start(bf16[128,256]{1,0:T(8,128)(2,1)S(1)} %pad_maximum_fusion.8), channel_id=1, source_target_pairs={{0,16},{4,20},{8,24},{12,28},{16,32},{20,36},{24,40},{28,44},{32,4... | collective-permute-start | bytes 196616 | tf_op jit(solution)/shard_map/ppermute | solution.py:22
  90.5 5.0 %collective-permute-start.11 = (bf16[128,256]{1,0:T(8,128)(2,1)S(1)}, bf16[128,256]{1,0:T(8,128)(2,1)S(1)}, u32[]{:S(2)}, u32[]{:S(2)}) collective-permute-start(bf16[128,256]{1,0:T(8,128)(2,1)S(1)} %pad_maximum_fusion.8), channel_id=1, source_target_pairs={{0,8},{4,12},{8,16},{12,20},{16,24},{20,28},{24,32},{28,36},{32,40... | collective-permute-start | bytes 196616 | tf_op jit(solution)/shard_map/ppermute | solution.py:22
  95.6 20.1 %collective-permute-start.12 = (bf16[640,256]{1,0:T(8,128)(2,1)S(1)}, bf16[640,256]{1,0:T(8,128)(2,1)S(1)}, u32[]{:S(2)}, u32[]{:S(2)}) collective-permute-start(bf16[640,256]{1,0:T(8,128)(2,1)S(1)} %get-tuple-element.39), channel_id=1, source_target_pairs={{0,4},{4,0},{1,5},{5,1},{2,6},{6,2},{3,7},{7,3},{8,12},{12,8},{9,1... | collective-permute-start | bytes 983048 | tf_op jit(solution)/shard_map/ppermute | solution.py:17
  101.0 29.9 %all-to-all-start.1 = ((bf16[128,8,128]{2,1,0:T(8,128)(2,1)}), bf16[128,8,128]{2,1,0:T(8,128)(2,1)S(1)}, u32[]{:S(2)}, u32[]{:S(2)}) async-start(bf16[128,8,128]{2,1,0:T(8,128)(2,1)} %fusion.22), calls=%async_computation.1 | async-start | bytes 524288 | tf_op jit(solution)/shard_map/all_to_all | solution.py:170
  116.4 1.9 %copy-start.1 = (bf16[4,8,4,24,512]{4,3,2,1,0:T(8,128)(2,1)S(1)}, bf16[4,8,4,24,512]{4,3,2,1,0:T(8,128)(2,1)}, u32[]{:S(2)}) copy-start(bf16[4,8,4,24,512]{4,3,2,1,0:T(8,128)(2,1)} %copy-done) | copy-start | bytes 9437188
  131.4 14.2 %copy-start.11 = (s32[96]{0:T(128)S(1)}, s32[96]{0:T(128)}, u32[]{:S(2)}) copy-start(s32[96]{0:T(128)} %param.15) | copy-start | bytes 1156
  132.5 12.9 %all-to-all-start.2 = ((bf16[4,128,512]{2,1,0:T(8,128)(2,1)}), bf16[4,128,512]{2,1,0:T(8,128)(2,1)S(1)}, u32[]{:S(2)}, u32[]{:S(2)}) async-start(bf16[4,128,512]{2,1,0:T(8,128)(2,1)} %pad_maximum_fusion.2), calls=%async_computation.2 | async-start | bytes 1048576 | tf_op jit(solution)/shard_map/all_to_all | solution.py:247

commit v4 on v2

--- a/solution.py
+++ b/solution.py
@@ -36,13 +36,17 @@
         jnp.broadcast_to(chunk[None], (members,) + chunk.shape), line, 0, 0, tiled=True
     )
     below = ring(own[:half], ("yh", "yl"), 1)
+    own_swapped = swap(own)
     above = ring(own[half:], ("yh", "yl"), -1)
-    own_swapped = swap(own)
-    sides = jnp.concatenate([below, above], axis=0)
-    sides_swapped = swap(sides)
-    shape = (n_zh, members // n_zh) + chunk.shape
-    pieces = [piece.reshape(shape) for piece in (own, sides, own_swapped, sides_swapped)]
-    return jnp.stack(pieces, axis=1)
+    below_swapped = swap(below)
+    above_swapped = swap(above)
+    shape = (n_zh // 2, members // n_zh) + chunk.shape
+    first = [own[:half], below, own_swapped[:half], below_swapped]
+    second = [own[half:], above, own_swapped[half:], above_swapped]
+    return jnp.concatenate(
+        [jnp.stack([part.reshape(shape) for part in parts], axis=1) for parts in (first, second)],
+        axis=0,
+    )
 
 
 def block_places(rows, offset, stacked):

time: 135 us -> 134 us (level)
  waiting for transfers between devices: 37.5 us -> 30.3 us
  other arithmetic: 9.92 us -> 14.5 us
  matrix products: 9.39 us -> 11.4 us
  local copies, waits for them, and re-layouts: 8.18 us -> 6.45 us
    ppermute x3 -> x4, starting transfers between devices: 12.7 us -> 16.2 us  [swap(): return lax.ppermute(x, 'c', [(0, 1), (1, 0)])]
    all_to_all x1, waiting for transfers between devices: 12.1 us -> 9.28 us  [gather_rows(): lax.all_to_all(jnp.broadcast_to(chunk[None], (members,) + chunk.shape), l...]
    concatenate x2, other arithmetic: 0.14 us -> 2.27 us  [place(): jnp.concatenate([jnp.dot(normed[:, k * block_width:(k + 1) * block_width]...]
    dot_general x8, matrix products: 3.39 us -> 5.42 us  [place(): jnp.dot(normed[:, k * block_width:(k + 1) * block_width], pick, preferred...]
    ppermute x2, waiting for transfers between devices: 1.98 us -> 0.01 us  [ring(): return lax.ppermute(x, axes, [(i, (i + step) % size) for i in range(size)])]
    concatenate x0 -> x1, other arithmetic: none -> 1.76 us  [gather_rows(): jnp.concatenate([jnp.stack([part.reshape(shape) for part in parts], axis=...]
    unnamed x36 -> x31, local copies, waits for them, and re-layouts: 3.7 us -> 2.69 us
  transfers between devices with their start and end apart: 12 -> 13, of which waited for: 6 -> 5; matrix products, arithmetic and copies ran while one was open for 13% -> 16% of each run, Pallas kernels for 0% -> 0%
where the time goes in v4:
time: 134 us; the launch traced here: 133 us
  starting transfers between devices  66.9 us (50%)
  waiting for transfers between devices  30.3 us (23%)
  other arithmetic  14.5 us (11%)
  matrix products  11.4 us (9%)
  local copies, waits for them, and re-layouts  6.45 us (5%)
  between operations  3.79 us (3%)
    all_to_all x1, starting transfers between devices, gather_rows(): lax.all_to_all(jnp.broadcast_to(chunk[None], (members,) + chunk.shape), l...  16.5 us
    ppermute x4, starting transfers between devices, swap(): return lax.ppermute(x, 'c', [(0, 1), (1, 0)])  16.2 us
    ppermute x4, starting transfers between devices, earlier(): lax.ppermute(x, TOK, [(i, i + distance) for i in range(size - distance)])  14.6 us
    all_to_all x1, waiting for transfers between devices, layer(): incoming = lax.all_to_all(outgoing, TOK, 0, 0, tiled=True)  10.4 us
    all_to_all x1, starting transfers between devices, layer(): incoming = lax.all_to_all(outgoing, TOK, 0, 0, tiled=True)  10.3 us
    all_to_all x1, waiting for transfers between devices, gather_rows(): lax.all_to_all(jnp.broadcast_to(chunk[None], (members,) + chunk.shape), l...  9.28 us
    all_to_all x1, waiting for transfers between devices, layer(): arrived = lax.all_to_all(sending, 'head', 0, 0, tiled=True)  8.92 us
    dot_general x8, matrix products, place(): jnp.dot(normed[:, k * block_width:(k + 1) * block_width], pick, preferred...  5.42 us
  transfers between devices with their start and end apart: 13, of which 5 were waited for; matrix products, arithmetic and copies ran while one was open for 16% of the time, Pallas kernels for 0%

profile of v4, /device:TPU:1, one launch (start us, length us, event | category | flops | bytes accessed | tf_op | source)
XLA Modules:
  0.0 133.3 jit_solution(8879585043241035378)
XLA Ops:
  0.6 0.8 fusion.180
  1.4 0.7 maximum_maximum_fusion.1
  2.1 0.9 broadcast_in_dim.43
  3.1 16.5 %all-to-all-start = ((bf16[32,24,512]{2,1,0:T(8,128)(2,1)}), bf16[32,24,512]{2,1,0:T(8,128)(2,1)S(1)}, u32[]{:S(2)}, u32[]{:S(2)}) async-start(bf16[32,24,512]{2,1,0:T(8,128)(2,1)} %broadcast_in_dim.43), calls=%async_computation | async-start | bytes 1572864 | tf_op jit(solution)/shard_map/all_to_all | solution.py:35
  21.4 1.0 fusion.14
  22.4 1.0 fusion.15
  23.8 0.6 fusion.169
  25.0 1.4 %fusion.165 = (s32[]{:T(128)}, s32[]{:T(128)}, s32[]{:T(128)}, s32[]{:T(128)}, s32[31]{0:T(128)S(1)}) fusion(s32[31]{0:T(128)S(1)} %copy-done.10, s32[]{:T(128)} %fusion.169, s32[]{:T(128)S(6)} %add.399, s32[31]{0:T(128)S(1)} %reduce.2), kind=kLoop, calls=%fused_computation.267 | loop fusion | flops 337 | bytes 396 | tf_op jit(solution)/shard_map/reduce_sum | solution.py:143
  28.4 1.0 fusion.92
  29.4 1.3 subtract_select_fusion
  30.7 1.0 fusion.16
  31.7 1.0 fusion.17
  32.9 1.0 pad_maximum_fusion.1
  34.2 9.3 %all-to-all-done = bf16[32,24,512]{2,1,0:T(8,128)(2,1)S(1)} async-done(((bf16[32,24,512]{2,1,0:T(8,128)(2,1)}), bf16[32,24,512]{2,1,0:T(8,128)(2,1)S(1)}, u32[]{:S(2)}, u32[]{:S(2)}) %all-to-all-start) | async-done | bytes 786464 | tf_op jit(solution)/shard_map/all_to_all | solution.py:35
  43.5 2.8 %collective-permute-start.3 = (bf16[16,24,512]{2,1,0:T(8,128)(2,1)S(1)}, bf16[16,24,512]{2,1,0:T(8,128)(2,1)}, u32[]{:S(2)}, u32[]{:S(2)}) collective-permute-start(bf16[16,24,512]{2,1,0:T(8,128)(2,1)S(1)} %get-tuple-element.24), channel_id=1, source_target_pairs={{0,56},{8,0},{16,8},{24,16},{32,24},{40,32},{48,40},{56,48},{1,57}... | collective-permute-start | bytes 1179656 | tf_op jit(solution)/shard_map/ppermute | solution.py:18
  46.3 2.5 %collective-permute-start = (bf16[16,24,512]{2,1,0:T(8,128)(2,1)S(1)}, bf16[16,24,512]{2,1,0:T(8,128)(2,1)}, u32[]{:S(2)}, u32[]{:S(2)}) collective-permute-start(bf16[16,24,512]{2,1,0:T(8,128)(2,1)S(1)} %get-tuple-element.23), channel_id=1, source_target_pairs={{0,8},{8,16},{16,24},{24,32},{32,40},{40,48},{48,56},{56,0},{1,9},... | collective-permute-start | bytes 1179656 | tf_op jit(solution)/shard_map/ppermute | solution.py:18
  48.8 5.5 %collective-permute-start.1 = (bf16[32,24,512]{2,1,0:T(8,128)(2,1)S(1)}, bf16[32,24,512]{2,1,0:T(8,128)(2,1)}, u32[]{:S(2)}, u32[]{:S(2)}) collective-permute-start(bf16[32,24,512]{2,1,0:T(8,128)(2,1)S(1)} %all-to-all-done), channel_id=1, source_target_pairs={{0,4},{4,0},{1,5},{5,1},{2,6},{6,2},{3,7},{7,3},{8,12},{12,8},{9,1... | collective-permute-start | bytes 2359304 | tf_op jit(solution)/shard_map/ppermute | solution.py:22
  54.3 0.9 iota_compare_fusion.26
  55.1 1.3 pad_maximum_fusion
  56.4 2.5 %collective-permute-start.4 = (bf16[16,24,512]{2,1,0:T(8,128)(2,1)}, bf16[16,24,512]{2,1,0:T(8,128)(2,1)}, u32[]{:S(2)}, u32[]{:S(2)}) collective-permute-start(bf16[16,24,512]{2,1,0:T(8,128)(2,1)} %collective-permute-done.3), channel_id=1, source_target_pairs={{0,4},{4,0},{1,5},{5,1},{2,6},{6,2},{3,7},{7,3},{8,12},{12,8},{9,1... | collective-permute-start | bytes 1179656 | tf_op jit(solution)/shard_map/ppermute | solution.py:22
  59.0 4.0 %collective-permute-start.2 = (bf16[16,24,512]{2,1,0:T(8,128)(2,1)}, bf16[16,24,512]{2,1,0:T(8,128)(2,1)}, u32[]{:S(2)}, u32[]{:S(2)}) collective-permute-start(bf16[16,24,512]{2,1,0:T(8,128)(2,1)} %collective-permute-done), channel_id=1, source_target_pairs={{0,4},{4,0},{1,5},{5,1},{2,6},{6,2},{3,7},{7,3},{8,12},{12,8},{9,1... | collective-permute-start | bytes 1179656 | tf_op jit(solution)/shard_map/ppermute | solution.py:22
  63.0 0.9 iota_compare_fusion.27
  63.8 1.2 fusion.175
  65.0 1.8 %maximum_maximum_fusion = bf16[4,4,8,24,512]{4,3,2,1,0:T(8,128)(2,1)S(1)} fusion(bf16[2,1,8,24,512]{4,3,2,1,0:T(8,128)(2,1)} %bitcast.10, bf16[2,1,8,24,512]{4,3,2,1,0:T(8,128)(2,1)S(1)} %bitcast.51, bf16[2,1,8,24,512]{4,3,2,1,0:T(8,128)(2,1)} %bitcast.8, bf16[2,1,8,24,512]{4,3,2,1,0:T(8,128)(2,1)S(1)} %bitcast.49, bf16[2,1,8,24,512]{4,3,2,1,0:T(8,128)(2,1)} %bitcast.6, ...), kind=kLoop, calls=%fused_computation.1 | loop fusion | flops 11010048 | bytes 6291456 | tf_op jit(solution)/shard_map/concatenate | solution.py:46
  66.8 0.4 convolution_convert_fusion.7
  67.2 0.6 fusion.182
  67.8 0.6 copy-done
  68.9 5.0 %collective-permute-start.5 = (bf16[128,256]{1,0:T(8,128)(2,1)S(1)}, bf16[128,256]{1,0:T(8,128)(2,1)S(1)}, u32[]{:S(2)}, u32[]{:S(2)}) collective-permute-start(bf16[128,256]{1,0:T(8,128)(2,1)S(1)} %pad_maximum_fusion.7), channel_id=1, source_target_pairs={{0,32},{4,36},{8,40},{12,44},{16,48},{20,52},{24,56},{28,60},{32,6... | collective-permute-start | bytes 196616 | tf_op jit(solution)/shard_map/ppermute | solution.py:27
  74.0 2.8 %collective-permute-start.6 = (bf16[128,256]{1,0:T(8,128)(2,1)S(1)}, bf16[128,256]{1,0:T(8,128)(2,1)S(1)}, u32[]{:S(2)}, u32[]{:S(2)}) collective-permute-start(bf16[128,256]{1,0:T(8,128)(2,1)S(1)} %pad_maximum_fusion.7), channel_id=1, source_target_pairs={{0,24},{4,28},{8,32},{12,36},{16,40},{20,44},{24,48},{28,52},{32,5... | collective-permute-start | bytes 196616 | tf_op jit(solution)/shard_map/ppermute | solution.py:27
  76.8 4.3 %collective-permute-start.7 = (bf16[128,256]{1,0:T(8,128)(2,1)S(1)}, bf16[128,256]{1,0:T(8,128)(2,1)S(1)}, u32[]{:S(2)}, u32[]{:S(2)}) collective-permute-start(bf16[128,256]{1,0:T(8,128)(2,1)S(1)} %pad_maximum_fusion.7), channel_id=1, source_target_pairs={{0,16},{4,20},{8,24},{12,28},{16,32},{20,36},{24,40},{28,44},{32,4... | collective-permute-start | bytes 196616 | tf_op jit(solution)/shard_map/ppermute | solution.py:27
  81.1 2.5 %collective-permute-start.8 = (bf16[128,256]{1,0:T(8,128)(2,1)S(1)}, bf16[128,256]{1,0:T(8,128)(2,1)S(1)}, u32[]{:S(2)}, u32[]{:S(2)}) collective-permute-start(bf16[128,256]{1,0:T(8,128)(2,1)S(1)} %pad_maximum_fusion.7), channel_id=1, source_target_pairs={{0,8},{4,12},{8,16},{12,20},{16,24},{20,28},{24,32},{28,36},{32,40... | collective-permute-start | bytes 196616 | tf_op jit(solution)/shard_map/ppermute | solution.py:27
  83.7 0.8 collective-permute-done.7
  84.5 0.8 collective-permute-done.8
  85.4 4.3 %collective-permute-start.9 = (bf16[640,256]{1,0:T(8,128)(2,1)S(1)}, bf16[640,256]{1,0:T(8,128)(2,1)S(1)}, u32[]{:S(2)}, u32[]{:S(2)}) collective-permute-start(bf16[640,256]{1,0:T(8,128)(2,1)S(1)} %get-tuple-element.41), channel_id=1, source_target_pairs={{0,4},{4,0},{1,5},{5,1},{2,6},{6,2},{3,7},{7,3},{8,12},{12,8},{9,1... | collective-permute-start | bytes 983048 | tf_op jit(solution)/shard_map/ppermute | solution.py:22
  89.8 1.1 fusion.22
  90.9 10.3 %all-to-all-start.1 = ((bf16[128,8,128]{2,1,0:T(8,128)(2,1)}), bf16[128,8,128]{2,1,0:T(8,128)(2,1)S(1)}, u32[]{:S(2)}, u32[]{:S(2)}) async-start(bf16[128,8,128]{2,1,0:T(8,128)(2,1)} %fusion.22), calls=%async_computation.1 | async-start | bytes 524288 | tf_op jit(solution)/shard_map/all_to_all | solution.py:158
  101.4 0.6 fusion.181
  101.9 0.4 fusion.2
  102.4 0.5 fusion.23
  102.9 0.9 copy-done.1
  103.8 0.9 convolution_convert_fusion
  106.0 10.4 %all-to-all-done.1 = bf16[128,8,128]{2,1,0:T(8,128)(2,1)S(1)} async-done(((bf16[128,8,128]{2,1,0:T(8,128)(2,1)}), bf16[128,8,128]{2,1,0:T(8,128)(2,1)S(1)}, u32[]{:S(2)}, u32[]{:S(2)}) %all-to-all-start.1) | async-done | bytes 262176 | tf_op jit(solution)/shard_map/all_to_all | solution.py:158
  117.1 0.9 pad_maximum_fusion.2
  117.9 4.0 %all-to-all-start.2 = ((bf16[4,128,512]{2,1,0:T(8,128)(2,1)}), bf16[4,128,512]{2,1,0:T(8,128)(2,1)S(1)}, u32[]{:S(2)}, u32[]{:S(2)}) async-start(bf16[4,128,512]{2,1,0:T(8,128)(2,1)} %pad_maximum_fusion.2), calls=%async_computation.2 | async-start | bytes 1048576 | tf_op jit(solution)/shard_map/all_to_all | solution.py:235
  122.0 8.9 %all-to-all-done.2 = bf16[4,128,512]{2,1,0:T(8,128)(2,1)S(1)} async-done(((bf16[4,128,512]{2,1,0:T(8,128)(2,1)}), bf16[4,128,512]{2,1,0:T(8,128)(2,1)S(1)}, u32[]{:S(2)}, u32[]{:S(2)}) %all-to-all-start.2) | async-done | bytes 524320 | tf_op jit(solution)/shard_map/all_to_all | solution.py:235
  131.1 0.3 fusion.4
  131.5 1.1 copy.37
  132.6 0.7 add_convert_fusion
  (83 shorter events, 5.7 us)
Async XLA Ops:
  0.6 19.0 %copy-start.9 = (bf16[1536]{0:T(1024)(128)(2,1)S(1)}, bf16[1536]{0:T(1024)(128)(2,1)}, u32[]{:S(2)}) copy-start(bf16[1536]{0:T(1024)(128)(2,1)} %param.9) | copy-start | bytes 9220
  0.6 19.0 %copy-start.2 = (bf16[128,1536]{1,0:T(8,128)(2,1)S(1)}, bf16[128,1536]{1,0:T(8,128)(2,1)}, u32[]{:S(2)}) copy-start(bf16[128,1536]{1,0:T(8,128)(2,1)} %param.8) | copy-start | bytes 1179652
  3.1 40.4 %all-to-all-start = ((bf16[32,24,512]{2,1,0:T(8,128)(2,1)}), bf16[32,24,512]{2,1,0:T(8,128)(2,1)S(1)}, u32[]{:S(2)}, u32[]{:S(2)}) async-start(bf16[32,24,512]{2,1,0:T(8,128)(2,1)} %broadcast_in_dim.43), calls=%async_computation | async-start | bytes 1572864 | tf_op jit(solution)/shard_map/all_to_all | solution.py:35
  20.0 3.5 %copy-start.10 = (s32[31]{0:T(128)S(1)}, s32[31]{0:T(128)}, u32[]{:S(2)}) copy-start(s32[31]{0:T(128)} %param.14) | copy-start | bytes 376
  20.0 7.1 %copy-start.12 = (s32[128]{0:T(128)S(1)}, s32[128]{0:T(128)}, u32[]{:S(2)}) copy-start(s32[128]{0:T(128)} %param.13) | copy-start | bytes 1540
  43.5 12.9 %collective-permute-start.3 = (bf16[16,24,512]{2,1,0:T(8,128)(2,1)S(1)}, bf16[16,24,512]{2,1,0:T(8,128)(2,1)}, u32[]{:S(2)}, u32[]{:S(2)}) collective-permute-start(bf16[16,24,512]{2,1,0:T(8,128)(2,1)S(1)} %get-tuple-element.24), channel_id=1, source_target_pairs={{0,56},{8,0},{16,8},{24,16},{32,24},{40,32},{48,40},{56,48},{1,57}... | collective-permute-start | bytes 1179656 | tf_op jit(solution)/shard_map/ppermute | solution.py:18
  46.3 12.6 %collective-permute-start = (bf16[16,24,512]{2,1,0:T(8,128)(2,1)S(1)}, bf16[16,24,512]{2,1,0:T(8,128)(2,1)}, u32[]{:S(2)}, u32[]{:S(2)}) collective-permute-start(bf16[16,24,512]{2,1,0:T(8,128)(2,1)S(1)} %get-tuple-element.23), channel_id=1, source_target_pairs={{0,8},{8,16},{16,24},{24,32},{32,40},{40,48},{48,56},{56,0},{1,9},... | collective-permute-start | bytes 1179656 | tf_op jit(solution)/shard_map/ppermute | solution.py:18
  48.8 15.0 %collective-permute-start.1 = (bf16[32,24,512]{2,1,0:T(8,128)(2,1)S(1)}, bf16[32,24,512]{2,1,0:T(8,128)(2,1)}, u32[]{:S(2)}, u32[]{:S(2)}) collective-permute-start(bf16[32,24,512]{2,1,0:T(8,128)(2,1)S(1)} %all-to-all-done), channel_id=1, source_target_pairs={{0,4},{4,0},{1,5},{5,1},{2,6},{6,2},{3,7},{7,3},{8,12},{12,8},{9,1... | collective-permute-start | bytes 2359304 | tf_op jit(solution)/shard_map/ppermute | solution.py:22
  56.4 8.6 %collective-permute-start.4 = (bf16[16,24,512]{2,1,0:T(8,128)(2,1)}, bf16[16,24,512]{2,1,0:T(8,128)(2,1)}, u32[]{:S(2)}, u32[]{:S(2)}) collective-permute-start(bf16[16,24,512]{2,1,0:T(8,128)(2,1)} %collective-permute-done.3), channel_id=1, source_target_pairs={{0,4},{4,0},{1,5},{5,1},{2,6},{6,2},{3,7},{7,3},{8,12},{12,8},{9,1... | collective-permute-start | bytes 1179656 | tf_op jit(solution)/shard_map/ppermute | solution.py:22
  59.0 6.1 %collective-permute-start.2 = (bf16[16,24,512]{2,1,0:T(8,128)(2,1)}, bf16[16,24,512]{2,1,0:T(8,128)(2,1)}, u32[]{:S(2)}, u32[]{:S(2)}) collective-permute-start(bf16[16,24,512]{2,1,0:T(8,128)(2,1)} %collective-permute-done), channel_id=1, source_target_pairs={{0,4},{4,0},{1,5},{5,1},{2,6},{6,2},{3,7},{7,3},{8,12},{12,8},{9,1... | collective-permute-start | bytes 1179656 | tf_op jit(solution)/shard_map/ppermute | solution.py:22
  65.0 1.8 %copy-start.3 = (bf16[128,3072]{1,0:T(8,128)(2,1)S(1)}, bf16[128,3072]{1,0:T(8,128)(2,1)}, u32[]{:S(2)}) copy-start(bf16[128,3072]{1,0:T(8,128)(2,1)} %pad_maximum_fusion.1) | copy-start | bytes 2359300
  66.8 1.6 %copy-start = (bf16[4,4,8,24,512]{4,3,2,1,0:T(8,128)(2,1)}, bf16[4,4,8,24,512]{4,3,2,1,0:T(8,128)(2,1)S(1)}, u32[]{:S(2)}) copy-start(bf16[4,4,8,24,512]{4,3,2,1,0:T(8,128)(2,1)S(1)} %maximum_maximum_fusion) | copy-start | bytes 9437188
  67.2 1.4 %copy-start.4 = (f32[128,64]{1,0:T(8,128)S(1)}, f32[128,64]{1,0:T(8,128)}, u32[]{:S(2)}) copy-start(f32[128,64]{1,0:T(8,128)} %get-tuple-element.59) | copy-start | bytes 98308
  67.2 1.4 %copy-start.5 = (f32[128,64]{1,0:T(8,128)S(1)}, f32[128,64]{1,0:T(8,128)}, u32[]{:S(2)}) copy-start(f32[128,64]{1,0:T(8,128)} %get-tuple-element.57) | copy-start | bytes 98308
  67.2 1.4 %copy-start.6 = (f32[128,64]{1,0:T(8,128)S(1)}, f32[128,64]{1,0:T(8,128)}, u32[]{:S(2)}) copy-start(f32[128,64]{1,0:T(8,128)} %get-tuple-element.58) | copy-start | bytes 98308
  68.4 21.4 %copy-start.7 = (pred[1024,128]{1,0:T(32,128)(4,1)S(1)}, pred[1024,128]{1,0:T(32,128)(4,1)}, u32[]{:S(2)}) copy-start(pred[1024,128]{1,0:T(32,128)(4,1)} %iota_compare_fusion.26) | copy-start | bytes 393220
  68.4 21.4 %copy-start.8 = (pred[1024,128]{1,0:T(32,128)(4,1)S(1)}, pred[1024,128]{1,0:T(32,128)(4,1)}, u32[]{:S(2)}) copy-start(pred[1024,128]{1,0:T(32,128)(4,1)} %iota_compare_fusion.27) | copy-start | bytes 393220
  68.9 14.7 %collective-permute-start.5 = (bf16[128,256]{1,0:T(8,128)(2,1)S(1)}, bf16[128,256]{1,0:T(8,128)(2,1)S(1)}, u32[]{:S(2)}, u32[]{:S(2)}) collective-permute-start(bf16[128,256]{1,0:T(8,128)(2,1)S(1)} %pad_maximum_fusion.7), channel_id=1, source_target_pairs={{0,32},{4,36},{8,40},{12,44},{16,48},{20,52},{24,56},{28,60},{32,6... | collective-permute-start | bytes 196616 | tf_op jit(solution)/shard_map/ppermute | solution.py:27
  74.0 9.7 %collective-permute-start.6 = (bf16[128,256]{1,0:T(8,128)(2,1)S(1)}, bf16[128,256]{1,0:T(8,128)(2,1)S(1)}, u32[]{:S(2)}, u32[]{:S(2)}) collective-permute-start(bf16[128,256]{1,0:T(8,128)(2,1)S(1)} %pad_maximum_fusion.7), channel_id=1, source_target_pairs={{0,24},{4,28},{8,32},{12,36},{16,40},{20,44},{24,48},{28,52},{32,5... | collective-permute-start | bytes 196616 | tf_op jit(solution)/shard_map/ppermute | solution.py:27
  76.8 7.7 %collective-permute-start.7 = (bf16[128,256]{1,0:T(8,128)(2,1)S(1)}, bf16[128,256]{1,0:T(8,128)(2,1)S(1)}, u32[]{:S(2)}, u32[]{:S(2)}) collective-permute-start(bf16[128,256]{1,0:T(8,128)(2,1)S(1)} %pad_maximum_fusion.7), channel_id=1, source_target_pairs={{0,16},{4,20},{8,24},{12,28},{16,32},{20,36},{24,40},{28,44},{32,4... | collective-permute-start | bytes 196616 | tf_op jit(solution)/shard_map/ppermute | solution.py:27
  81.1 4.3 %collective-permute-start.8 = (bf16[128,256]{1,0:T(8,128)(2,1)S(1)}, bf16[128,256]{1,0:T(8,128)(2,1)S(1)}, u32[]{:S(2)}, u32[]{:S(2)}) collective-permute-start(bf16[128,256]{1,0:T(8,128)(2,1)S(1)} %pad_maximum_fusion.7), channel_id=1, source_target_pairs={{0,8},{4,12},{8,16},{12,20},{16,24},{20,28},{24,32},{28,36},{32,40... | collective-permute-start | bytes 196616 | tf_op jit(solution)/shard_map/ppermute | solution.py:27
  85.4 15.8 %collective-permute-start.9 = (bf16[640,256]{1,0:T(8,128)(2,1)S(1)}, bf16[640,256]{1,0:T(8,128)(2,1)S(1)}, u32[]{:S(2)}, u32[]{:S(2)}) collective-permute-start(bf16[640,256]{1,0:T(8,128)(2,1)S(1)} %get-tuple-element.41), channel_id=1, source_target_pairs={{0,4},{4,0},{1,5},{5,1},{2,6},{6,2},{3,7},{7,3},{8,12},{12,8},{9,1... | collective-permute-start | bytes 983048 | tf_op jit(solution)/shard_map/ppermute | solution.py:22
  90.9 25.5 %all-to-all-start.1 = ((bf16[128,8,128]{2,1,0:T(8,128)(2,1)}), bf16[128,8,128]{2,1,0:T(8,128)(2,1)S(1)}, u32[]{:S(2)}, u32[]{:S(2)}) async-start(bf16[128,8,128]{2,1,0:T(8,128)(2,1)} %fusion.22), calls=%async_computation.1 | async-start | bytes 524288 | tf_op jit(solution)/shard_map/all_to_all | solution.py:158
  101.9 1.9 %copy-start.1 = (bf16[4,4,8,24,512]{4,3,2,1,0:T(8,128)(2,1)S(1)}, bf16[4,4,8,24,512]{4,3,2,1,0:T(8,128)(2,1)}, u32[]{:S(2)}) copy-start(bf16[4,4,8,24,512]{4,3,2,1,0:T(8,128)(2,1)} %copy-done) | copy-start | bytes 9437188
  116.9 14.2 %copy-start.11 = (s32[96]{0:T(128)S(1)}, s32[96]{0:T(128)}, u32[]{:S(2)}) copy-start(s32[96]{0:T(128)} %param.15) | copy-start | bytes 1156
  117.9 12.9 %all-to-all-start.2 = ((bf16[4,128,512]{2,1,0:T(8,128)(2,1)}), bf16[4,128,512]{2,1,0:T(8,128)(2,1)S(1)}, u32[]{:S(2)}, u32[]{:S(2)}) async-start(bf16[4,128,512]{2,1,0:T(8,128)(2,1)} %pad_maximum_fusion.2), calls=%async_computation.2 | async-start | bytes 1048576 | tf_op jit(solution)/shard_map/all_to_all | solution.py:235
